TPU v7x, 32 devices: a whole 2x2x4 slice. The times are simulated.
32 devices in a mesh: row: 2 (over core), col: 4 (over y, x), mem: 4 (over z).
Axes of the slice: x: 2, y: 2, z: 4, core: 2. Of those that a mesh axis runs over, the one named last changes fastest.
Arguments:
- source_columns: bfloat16 [32768, 256], P(('mem', 'row', 'col')), parts along dimension 0, may hold values from -6 to 6
- tiles: bfloat16 [8, 4, 256, 128, 128], P(('mem', 'row'), 'col'), parts along dimension 0, may hold values from -0.15625 to 0.15625
- tile_index: int32 [8, 4, 256, 2], P(('mem', 'row'), 'col'), parts along dimension 0, may hold values from 0 to 31, as said below
- tile_count: int32 [8, 4], P(('mem', 'row'), 'col'), parts along dimension 0, may hold values from 32 to 256, as said below
Outputs:
- twice_coupled: bfloat16 [32768, 256], P(('mem', 'row', 'col')), parts along dimension 0
There are 4 independent parts, one for each index of `mem`. A program takes and returns all parts, laid end to end along the dimension named above; each array names one. Nothing has to cross between parts.
Inputs may be any that keep to these rules, and one draw needn't show every extreme that they name: `tile_index`: slots k * 32 to (k + 1) * 32 - 1 of a device name every local block-row exactly once in their first entry; the panel block-columns of one block-row on one device all differ. Block-row entries lie in 0 to 31, block-column entries in 0 to 15. `tile_count`: each count is a multiple of 32; in every draw some device has all 256 slots live.
All inputs are finite; a program needn't handle non-finite values.
Results may differ from a plain program's by a relative error of at most 0.0049.
Values may be sent and summed in bfloat16 or wider, within the bound.
No kernel may reach another device: no remote copies, remote signals or barrier semaphores. Data moves between devices by JAX's collectives and lax.ppermute only.
A program may use at most 128 MiB of HBM per device.

v0:
```python
import jax
import jax.numpy as jnp
from jax import lax
from jax.sharding import PartitionSpec as P

TILE_SIZE = 128
BLOCK_ROWS = 32


def sweep(totals, source, tiles3, index3, live_levels):

    def level(level_at, running):
        tile_set = lax.dynamic_index_in_dim(tiles3, level_at, 0, keepdims=False)
        index_set = lax.dynamic_index_in_dim(index3, level_at, 0, keepdims=False)
        order = (
            jnp.zeros((BLOCK_ROWS,), jnp.int32)
            .at[index_set[:, 0]]
            .set(jnp.arange(BLOCK_ROWS, dtype=jnp.int32))
        )
        blocks = source[index_set[:, 1][order]]
        product = jnp.einsum(
            "bij,bjn->bin", tile_set[order], blocks, preferred_element_type=jnp.float32
        )
        return running + product

    return lax.fori_loop(0, live_levels, level, totals)


def couple(values, tiles3, index3, live_levels):
    column_total = values.shape[1]
    start_totals = jnp.zeros((BLOCK_ROWS, TILE_SIZE, column_total), jnp.float32)
    gathered = lax.all_gather(values, "row", axis=0, tiled=True)
    blocks_all = gathered.reshape(-1, TILE_SIZE, column_total)
    totals = sweep(start_totals, blocks_all, tiles3, index3, live_levels)
    partial_rows = totals.reshape(-1, column_total)
    return lax.psum_scatter(partial_rows, "col", scatter_dimension=0, tiled=True).astype(
        jnp.bfloat16
    )


def local(source_columns, tiles, tile_index, tile_count):
    tiles3 = tiles.reshape(-1, BLOCK_ROWS, TILE_SIZE, TILE_SIZE)
    index3 = tile_index.reshape(-1, BLOCK_ROWS, 2)
    live_levels = tile_count.reshape(()) // BLOCK_ROWS
    once = couple(source_columns, tiles3, index3, live_levels)
    return couple(once, tiles3, index3, live_levels)


def solution(mesh):
    placed = (
        P(("mem", "row", "col"), None),
        P(("mem", "row"), "col", None, None, None),
        P(("mem", "row"), "col", None, None),
        P(("mem", "row"), "col"),
    )
    return jax.shard_map(
        local, mesh=mesh, in_specs=placed, out_specs=P(("mem", "row", "col"), None), check_vma=False
    )
```

profile of v0, /device:TPU:0, one launch (start us, length us, event | category | flops | bytes accessed | tf_op | source)
XLA Modules:
  0.0 317.5 jit_solution(7756922940259139396)
XLA Ops:
  6.5 0.7 all-gather.3.cloned.1.call-update
  8.0 0.8 reshape.49
  8.7 11.9 %all-gather.3.cloned.1.call-done = bf16[2048,256]{1,0:T(8,128)(2,1)} async-done(((bf16[1024,256]{1,0:T(8,128)(2,1)}), bf16[2048,256]{1,0:T(8,128)(2,1)}) %all-gather.3.cloned.1.call-update) | async-done | bytes 1048592 | tf_op jit(solution)/shard_map/all_gather | solution.py:32
  20.7 2.4 broadcast.62.clone
  23.1 10.4 %while.20 = (s32[]{:T(128)}, f32[32,128,256]{2,1,0:T(8,128)}, s32[]{:T(128)}, bf16[8,32,128,128]{3,2,1,0:T(8,128)(2,1)}, s32[8,32,2]{1,2,0:T(2,128)S(1)}, /*inde...) while((s32[]{:T(128)}, f32[32,128,256]{2,1,0:T(8,128)}, ...), condition=%wide.region_2.3_spmd, body=%wide.region_0.2_spmd.sunk | while | flops 269486368 | bytes 24128304 | solution.py:26
  23.1 0.7 scatter_custom_fusion.9
  23.8 0.7 gather_fusion.1
  24.6 0.7 gather_fusion.2
  25.2 1.3 dynamic-slice_bitcast_fusion.8
  26.6 1.7 gather_fusion
  28.2 5.2 %convolution_add_fusion.4 = f32[32,128,256]{2,1,0:T(8,128)} fusion(f32[32,128,256]{2,1,0:T(8,128)} %get-tuple-element.207, bf16[32,128,128]{2,1,0:T(8,128)(2,1)} %gather_fusion, bf16[32,128,256]{2,1,0:T(8,128)(2,1)S(1)} %gather_fusion.2), kind=kOutput, calls=%fused_computation.8.clone.1 | convolution fusion | flops 269484032 | bytes 11534336 | tf_op jit(solution)/shard_map/while/body/bij,bjn->bin/dot_general | solution.py:21
  33.6 125.6 %reduce-scatter.3.cloned.1.call-done = f32[1024,256]{1,0:T(8,128)} async-done(((f32[4096,256]{1,0:T(8,128)}), f32[1024,256]{1,0:T(8,128)}) %reduce-scatter.3.cloned.1.call-update) | async-done | bytes 1048592 | tf_op jit(solution)/shard_map/reduce_scatter | solution.py:36
  159.1 2.1 convert_element_type.6
  161.3 9.1 %all-gather.5.cloned.1.call-done = bf16[2048,256]{1,0:T(8,128)(2,1)} async-done(((bf16[1024,256]{1,0:T(8,128)(2,1)}), bf16[2048,256]{1,0:T(8,128)(2,1)}) %all-gather.5.cloned.1.call-update) | async-done | bytes 1048592 | tf_op jit(solution)/shard_map/all_gather | solution.py:32
  170.4 2.4 broadcast.62
  172.8 10.4 %while.21 = (s32[]{:T(128)}, f32[32,128,256]{2,1,0:T(8,128)}, s32[]{:T(128)}, bf16[8,32,128,128]{3,2,1,0:T(8,128)(2,1)}, s32[8,32,2]{1,2,0:T(2,128)S(1)}, /*inde...) while((s32[]{:T(128)}, f32[32,128,256]{2,1,0:T(8,128)}, ...), condition=%wide.region_6.7_spmd, body=%wide.region_4.6_spmd.sunk | while | flops 269486368 | bytes 24128304 | solution.py:26
  172.9 0.7 scatter_custom_fusion.11
  173.6 0.7 gather_fusion.4
  174.3 0.7 gather_fusion.5
  175.0 1.3 dynamic-slice_bitcast_fusion.10
  176.3 1.7 gather_fusion.3
  178.0 5.2 %convolution_add_fusion.5 = f32[32,128,256]{2,1,0:T(8,128)} fusion(f32[32,128,256]{2,1,0:T(8,128)} %get-tuple-element.234, bf16[32,128,128]{2,1,0:T(8,128)(2,1)} %gather_fusion.3, bf16[32,128,256]{2,1,0:T(8,128)(2,1)S(1)} %gather_fusion.5), kind=kOutput, calls=%fused_computation.21.clone.1 | convolution fusion | flops 269484032 | bytes 11534336 | tf_op jit(solution)/shard_map/while/body/bij,bjn->bin/dot_general | solution.py:21
  183.2 125.7 %reduce-scatter.5.cloned.1.call-done = f32[1024,256]{1,0:T(8,128)} async-done(((f32[4096,256]{1,0:T(8,128)}), f32[1024,256]{1,0:T(8,128)}) %reduce-scatter.5.cloned.1.call-update) | async-done | bytes 1048592 | tf_op jit(solution)/shard_map/reduce_scatter | solution.py:36
  308.9 2.1 convert_element_type.7
  (30 shorter events, 0.3 us)
Async XLA Ops:
  6.5 14.1 %all-gather.3.cloned.1.call-start = ((), (), s32[]{:S(2)}) async-start(), calls=%async_computation.2 | async-start | bytes 1572864 | tf_op jit(solution)/shard_map/all_gather | solution.py:32
  7.3 151.9 %reduce-scatter.3.cloned.1.call-start = ((), (), s32[]{:S(2)}) async-start(), calls=%async_computation.3 | async-start | bytes 5242880 | tf_op jit(solution)/shard_map/reduce_scatter | solution.py:36
  20.7 2.4 copy-start
  28.2 5.2 %copy-start.1 = (bf16[2048,256]{1,0:T(8,128)(2,1)S(1)}, bf16[2048,256]{1,0:T(8,128)(2,1)}, u32[]{:S(2)}) copy-start(bf16[2048,256]{1,0:T(8,128)(2,1)} %get-tuple-element.269) | copy-start | bytes 3145732 | tf_op jit(solution)/shard_map/while
  33.5 136.9 %all-gather.5.cloned.1.call-start = ((), (), s32[]{:S(2)}) async-start(), calls=%async_computation.4 | async-start | bytes 1572864 | tf_op jit(solution)/shard_map/all_gather | solution.py:32
  161.2 147.7 %reduce-scatter.5.cloned.1.call-start = ((), (), s32[]{:S(2)}) async-start(), calls=%async_computation.5 | async-start | bytes 5242880 | tf_op jit(solution)/shard_map/reduce_scatter | solution.py:36
  170.4 2.4 copy-start.2
  178.0 5.2 %copy-start.3 = (bf16[2048,256]{1,0:T(8,128)(2,1)S(1)}, bf16[2048,256]{1,0:T(8,128)(2,1)}, u32[]{:S(2)}) copy-start(bf16[2048,256]{1,0:T(8,128)(2,1)} %get-tuple-element.280) | copy-start | bytes 3145732 | tf_op jit(solution)/shard_map/while
Sparse Core Ops, SparseCore 0:
  8.9 11.7 all-gather.2
  33.6 125.4 reduce-scatter.2
  161.4 9.0 all-gather.4
  183.4 125.4 reduce-scatter.4
where the time goes:
time: 319 us; the launch traced here: 318 us
  waiting for transfers between devices  273 us (86%)
  local copies, waits for them, and re-layouts  15.7 us (5%)
  between operations  13.8 us (4%)
  matrix products  10.5 us (3%)
  other arithmetic  4.2 us (1%)
    reduce_scatter x2, waiting for transfers between devices, couple(): lax.psum_scatter(partial_rows, 'col', scatter_dimension=0, tiled=True)  251 us
    all_gather x2, waiting for transfers between devices, couple(): gathered = lax.all_gather(values, 'row', axis=0, tiled=True)  21.1 us
    dot_general x2, matrix products, level(): jnp.einsum('bij,bjn->bin', tile_set[order], blocks, preferred_element_typ...  10.5 us
  transfers between devices with their start and end apart: 4, of which 4 were waited for; matrix products, arithmetic and copies ran while one was open for 0% of the time, Pallas kernels for 0%

commit v1 on v0

v1 whole, which is shorter than its diff:
```python
import functools

import jax
import jax.numpy as jnp
from jax import lax
from jax.experimental import pallas as pl
from jax.experimental.pallas import tpu as pltpu
from jax.sharding import PartitionSpec as P

TILE_SIZE = 128
BLOCK_ROWS = 32
COL_SHIFT = 16

QUARTERS = (3, 1, 2, 0)


def sweep_kernel(sources, outs_of_rows, *refs):
    table, tiles = refs[:2]
    source_refs = refs[2 : 2 + sources]
    out_refs = refs[2 + sources : -1]
    panel = refs[-1]
    at = 0
    for source in source_refs:
        panel[at : at + source.shape[0]] = source[...]
        at += source.shape[0]
    panel[at] = jnp.zeros_like(panel[at])
    levels = table.shape[1]
    first = 0
    for out, count in zip(out_refs, outs_of_rows):

        def row(b, carry, out=out, first=first):
            left, right = [], []
            for k in range(levels):
                entry = table[first + b, k]
                left.append(tiles[entry >> COL_SHIFT])
                right.append(panel[entry & ((1 << COL_SHIFT) - 1)])
            total = jnp.dot(
                jnp.concatenate(left, 1), jnp.concatenate(right, 0), preferred_element_type=jnp.float32
            )
            out[b] = total.astype(out.dtype)
            return carry

        lax.fori_loop(0, count, row, 0, unroll=4)
        first += count


def sweep(table, tiles, sources, outs):
    columns = sources[0].shape[-1]
    blocks = sum(s.shape[0] for s in sources)
    vmem = pl.BlockSpec(memory_space=pltpu.VMEM)
    return pl.pallas_call(
        functools.partial(sweep_kernel, len(sources), [n for n, _ in outs]),
        out_shape=[jax.ShapeDtypeStruct((n, TILE_SIZE, columns), dtype) for n, dtype in outs],
        in_specs=[pl.BlockSpec(memory_space=pltpu.SMEM)] + [vmem] * (1 + len(sources)),
        out_specs=[vmem] * len(outs),
        scratch_shapes=[pltpu.VMEM((blocks + 1, TILE_SIZE, columns), jnp.bfloat16)],
        compiler_params=pltpu.CompilerParams(vmem_limit_bytes=24 << 20),
    )(table, tiles, *sources)


def swap(values, mask, n_col):
    return lax.ppermute(values, "col", [(c, c ^ mask) for c in range(n_col)])


def row_table(tile_index, tile_count, n_row, n_col, blocks, own_first):
    index = tile_index.reshape(-1, BLOCK_ROWS, 2)
    levels = index.shape[0]
    rows, panel_block = index[..., 0], index[..., 1]
    if own_first:
        panel_block = panel_block ^ (lax.axis_index("row") * (BLOCK_ROWS // n_col))
    level = jnp.arange(levels, dtype=jnp.int32)[:, None]
    live = level * BLOCK_ROWS < tile_count.reshape(())
    slot = level * BLOCK_ROWS + jnp.arange(BLOCK_ROWS, dtype=jnp.int32)
    entry = (slot << COL_SHIFT) | jnp.where(live, panel_block, blocks)
    place = lax.axis_index("col")
    share = BLOCK_ROWS // n_col
    wanted = jnp.concatenate([(place ^ q) * share + jnp.arange(share, dtype=jnp.int32) for q in QUARTERS])
    hit = rows[None] == wanted[:, None, None]
    return jnp.sum(jnp.where(hit, entry[None], 0), axis=-1, dtype=jnp.int32)


def couple(values, table, tiles, n_row, n_col):
    share = BLOCK_ROWS // n_col
    half = share // 2
    f32, bf16 = jnp.float32, jnp.bfloat16
    blocks = values.reshape(share, TILE_SIZE, -1)
    if n_row == 2:
        sources = [blocks, lax.ppermute(blocks, "row", [(0, 1), (1, 0)])]
    else:
        sources = [lax.all_gather(blocks, "row", axis=0, tiled=True)]
    d_a, d_b = sweep(table[:share], tiles, sources, [(half, bf16), (half, bf16)])
    d_a, d_b = swap(d_a, 1, n_col), swap(d_b, 2, n_col)
    x_a, x_b, y_a, y_b = sweep(
        table[share : 3 * share], tiles, sources, [(half, bf16), (half, f32), (half, f32), (half, bf16)]
    )
    x_a, y_b = swap(x_a, 1, n_col), swap(y_b, 2, n_col)
    (own,) = sweep(table[3 * share :], tiles, sources, [(share, f32)])
    y_a = swap((y_a + d_a.astype(f32)).astype(bf16), 2, n_col)
    x_b = swap((x_b + d_b.astype(f32)).astype(bf16), 1, n_col)
    first = own[:half] + x_a.astype(f32) + y_a.astype(f32)
    second = own[half:] + y_b.astype(f32) + x_b.astype(f32)
    return jnp.concatenate([first, second], 0).astype(bf16).reshape(values.shape)


def local(n_row, n_col, source_columns, tiles, tile_index, tile_count):
    tiles = tiles.reshape(-1, TILE_SIZE, TILE_SIZE)
    blocks = n_row * BLOCK_ROWS // n_col
    table = row_table(tile_index, tile_count, n_row, n_col, blocks, n_row == 2)
    once = couple(source_columns, table, tiles, n_row, n_col)
    return couple(once, table, tiles, n_row, n_col)


def solution(mesh):
    n_row, n_col = mesh.shape["row"], mesh.shape["col"]
    assert n_col == 4
    placed = (
        P(("mem", "row", "col"), None),
        P(("mem", "row"), "col", None, None, None),
        P(("mem", "row"), "col", None, None),
        P(("mem", "row"), "col"),
    )
    return jax.shard_map(
        functools.partial(local, n_row, n_col),
        mesh=mesh,
        in_specs=placed,
        out_specs=P(("mem", "row", "col"), None),
        check_vma=False,
    )
```

time: 319 us -> 56.8 us (0.18)
  waiting for transfers between devices: 273 us -> 23.6 us
  starting transfers between devices: 0.12 us -> 13.9 us
  between operations: 13.8 us -> 0.8 us
  Pallas kernels: 0 us -> 10.6 us
  local copies, waits for them, and re-layouts: 15.7 us -> 5.19 us
  matrix products: 10.5 us -> 0 us
    reduce_scatter x2 -> x0, waiting for transfers between devices: 251 us -> none  [couple(): lax.psum_scatter(partial_rows, 'col', scatter_dimension=0, tiled=True)]
    ppermute x0 -> x14, waiting for transfers between devices: none -> 23.6 us  [the longest x12 21.7 us: swap(): return lax.ppermute(values, 'col', [(c, c ^ mask) for c in range(n_col)])]
    all_gather x2 -> x0, waiting for transfers between devices: 21.1 us -> none  [couple(): gathered = lax.all_gather(values, 'row', axis=0, tiled=True)]
    ppermute x0 -> x14, starting transfers between devices: none -> 13.9 us  [the longest x12 13.4 us: swap(): return lax.ppermute(values, 'col', [(c, c ^ mask) for c in range(n_col)])]
    pallas_call x0 -> x6, Pallas kernels: none -> 10.6 us  [sweep(): pl.pallas_call(functools.partial(sweep_kernel, len(sources), [n for n, _...]
    dot_general x2 -> x0, matrix products: 10.5 us -> none  [level(): jnp.einsum('bij,bjn->bin', tile_set[order], blocks, preferred_element_typ...]
    gather x6 -> x0, local copies, waits for them, and re-layouts: 6.13 us -> none  [the longest x2 3.37 us: level(): tile_set[order]]
    another operation x2 -> x0, local copies, waits for them, and re-layouts: 4.87 us -> none
  transfers between devices with their start and end apart: 4 -> 14, of which waited for: 4 -> 10; matrix products, arithmetic and copies ran while one was open for 0% -> 3% of each run, Pallas kernels for 0% -> 13%
where the time goes in v1:
time: 56.8 us; the launch traced here: 56.6 us
  waiting for transfers between devices  23.6 us (42%)
  starting transfers between devices  13.9 us (24%)
  Pallas kernels  10.6 us (19%)
  local copies, waits for them, and re-layouts  5.19 us (9%)
  other arithmetic  2.44 us (4%)
  between operations  0.8 us (1%)
    ppermute x12, waiting for transfers between devices, swap(): return lax.ppermute(values, 'col', [(c, c ^ mask) for c in range(n_col)])  21.7 us
    ppermute x12, starting transfers between devices, swap(): return lax.ppermute(values, 'col', [(c, c ^ mask) for c in range(n_col)])  13.4 us
    pallas_call x6, Pallas kernels, sweep(): pl.pallas_call(functools.partial(sweep_kernel, len(sources), [n for n, _...  10.6 us
    unnamed x8, local copies, waits for them, and re-layouts  4.43 us
    ppermute x2, waiting for transfers between devices, couple(): sources = [blocks, lax.ppermute(blocks, 'row', [(0, 1), (1, 0)])]  1.9 us
  transfers between devices with their start and end apart: 14, of which 10 were waited for; matrix products, arithmetic and copies ran while one was open for 3% of the time, Pallas kernels for 13%

profile of v1, /device:TPU:0, one launch (start us, length us, event | category | flops | bytes accessed | tf_op | source)
XLA Modules:
  0.0 56.6 jit_solution(12358728589604322498)
XLA Ops:
  2.8 3.4 %copy-done = bf16[1,1,256,128,128]{4,3,2,1,0:T(8,128)(2,1)S(1)} copy-done((bf16[1,1,256,128,128]{4,3,2,1,0:T(8,128)(2,1)S(1)}, bf16[1,1,256,128,128]{4,3,2,1,0:T(8,128)(2,1)}, u32[]{:S(2)}) %copy-start) | copy-done | bytes 8388632
  6.2 1.0 %copy-done.1 = bf16[1024,256]{1,0:T(8,128)(2,1)S(1)} copy-done((bf16[1024,256]{1,0:T(8,128)(2,1)S(1)}, bf16[1024,256]{1,0:T(8,128)(2,1)}, u32[]{:S(2)}) %copy-start.1) | copy-done | bytes 524312
  7.2 1.4 %shard_map.48 = (bf16[4,128,256]{2,1,0:T(8,128)(2,1)S(1)}, bf16[4,128,256]{2,1,0:T(8,128)(2,1)S(1)}) custom-call(s32[8,8]{1,0:T(8,128)S(1)} %get-tuple-element.33.refs_0_, bf16[256,128,128]{2,1,0:T(8,128)(2,1)S(1)} %bitcast.15, bf16[8,128,256]{2,1,0:T(8,128)(2,1)S(1)} %bitcast.24, bf16[8,128,256]{2,1,0:T(8,128)(2,1)S(1)} %collective-permute-done.refs_3_), custom_call_target="tpu_custom_call" | custom-call | tf_op jit(solution)/shard_map/pallas_call | solution.py:51
  8.6 2.6 %collective-permute-start.2 = (bf16[4,128,256]{2,1,0:T(8,128)(2,1)S(1)}, bf16[4,128,256]{2,1,0:T(8,128)(2,1)S(1)}, u32[]{:S(2)}, u32[]{:S(2)}) collective-permute-start(bf16[4,128,256]{2,1,0:T(8,128)(2,1)S(1)} %get-tuple-element.19), channel_id=1, source_target_pairs={{0,4},{4,0},{8,12},{12,8},{1,5},{5,1},{9,13},{13,9},{2,6},{6,2},{1... | collective-permute-start | bytes 786440 | tf_op jit(solution)/shard_map/ppermute | solution.py:62
  11.2 1.5 %collective-permute-start.5 = (bf16[4,128,256]{2,1,0:T(8,128)(2,1)S(1)}, bf16[4,128,256]{2,1,0:T(8,128)(2,1)S(1)}, u32[]{:S(2)}, u32[]{:S(2)}) collective-permute-start(bf16[4,128,256]{2,1,0:T(8,128)(2,1)S(1)} %get-tuple-element.22), channel_id=1, source_target_pairs={{0,8},{4,12},{8,0},{12,4},{1,9},{5,13},{9,1},{13,5},{2,10},{6,14},... | collective-permute-start | bytes 786440 | tf_op jit(solution)/shard_map/ppermute | solution.py:62
  12.7 2.1 %shard_map.47 = (bf16[4,128,256]{2,1,0:T(8,128)(2,1)S(1)}, f32[4,128,256]{2,1,0:T(8,128)S(1)}, f32[4,128,256]{2,1,0:T(8,128)S(1)}, bf16[4,128,256]{2,1,0:T(8,128)(2,1)S(1)}) custom-call(s32[16,8]{1,0:T(8,128)S(1)} %slice.43.refs_0_, bf16[256,128,128]{2,1,0:T(8,128)(2,1)S(1)} %bitcast.16, bf16[8,128,256]{2,1,0:T(8,128)(2,1)S(1)} %bitcast.25, ...), custom_call_target="tpu_custom_call" | custom-call | tf_op jit(solution)/shard_map/pallas_call | solution.py:51
  15.5 2.9 %collective-permute-done.2 = bf16[4,128,256]{2,1,0:T(8,128)(2,1)S(1)} collective-permute-done((bf16[4,128,256]{2,1,0:T(8,128)(2,1)S(1)}, bf16[4,128,256]{2,1,0:T(8,128)(2,1)S(1)}, u32[]{:S(2)}, u32[]{:S(2)}) %collective-permute-start.2) | collective-permute-done | bytes 262176 | tf_op jit(solution)/shard_map/ppermute | solution.py:62
  18.4 2.0 %collective-permute-start.3 = (bf16[4,128,256]{2,1,0:T(8,128)(2,1)S(1)}, bf16[4,128,256]{2,1,0:T(8,128)(2,1)S(1)}, u32[]{:S(2)}, u32[]{:S(2)}) collective-permute-start(bf16[4,128,256]{2,1,0:T(8,128)(2,1)S(1)} %add_convert_fusion.3), channel_id=1, source_target_pairs={{0,8},{4,12},{8,0},{12,4},{1,9},{5,13},{9,1},{13,5},{2,10},{6,14},... | collective-permute-start | bytes 786440 | tf_op jit(solution)/shard_map/ppermute | solution.py:62
  20.6 1.6 %collective-permute-start.6 = (bf16[4,128,256]{2,1,0:T(8,128)(2,1)S(1)}, bf16[4,128,256]{2,1,0:T(8,128)(2,1)S(1)}, u32[]{:S(2)}, u32[]{:S(2)}) collective-permute-start(bf16[4,128,256]{2,1,0:T(8,128)(2,1)S(1)} %add_convert_fusion.2), channel_id=1, source_target_pairs={{0,4},{4,0},{8,12},{12,8},{1,5},{5,1},{9,13},{13,9},{2,6},{6,2},{1... | collective-permute-start | bytes 786440 | tf_op jit(solution)/shard_map/ppermute | solution.py:62
  22.1 1.7 %shard_map.46 = f32[8,128,256]{2,1,0:T(8,128)S(1)} custom-call(s32[8,8]{1,0:T(8,128)S(1)} %get-tuple-element.34.refs_0_, bf16[256,128,128]{2,1,0:T(8,128)(2,1)S(1)} %bitcast.19, bf16[8,128,256]{2,1,0:T(8,128)(2,1)S(1)} %bitcast.26, bf16[8,128,256]{2,1,0:T(8,128)(2,1)S(1)} %collective-permute-done.refs_3_), custom_call_target="tpu_custom_call" | custom-call | tf_op jit(solution)/shard_map/pallas_call | solution.py:51
  24.1 1.8 %collective-permute-done.4 = bf16[4,128,256]{2,1,0:T(8,128)(2,1)S(1)} collective-permute-done((bf16[4,128,256]{2,1,0:T(8,128)(2,1)S(1)}, bf16[4,128,256]{2,1,0:T(8,128)(2,1)S(1)}, u32[]{:S(2)}, u32[]{:S(2)}) %collective-permute-start.4) | collective-permute-done | bytes 262176 | tf_op jit(solution)/shard_map/ppermute | solution.py:62
  26.0 4.9 %collective-permute-done.3 = bf16[4,128,256]{2,1,0:T(8,128)(2,1)S(1)} collective-permute-done((bf16[4,128,256]{2,1,0:T(8,128)(2,1)S(1)}, bf16[4,128,256]{2,1,0:T(8,128)(2,1)S(1)}, u32[]{:S(2)}, u32[]{:S(2)}) %collective-permute-start.3) | collective-permute-done | bytes 262176 | tf_op jit(solution)/shard_map/ppermute | solution.py:62
  31.2 1.9 %collective-permute-done.7.refs_3_ = bf16[8,128,256]{2,1,0:T(8,128)(2,1)S(1)} collective-permute-done((bf16[8,128,256]{2,1,0:T(8,128)(2,1)S(1)}, bf16[8,128,256]{2,1,0:T(8,128)(2,1)S(1)}, u32[]{:S(2)}, u32[]{:S(2)}) %collective-permute-start.7) | collective-permute-done | bytes 524320 | tf_op jit(solution)/shard_map/ppermute | solution.py:88
  33.1 1.5 %shard_map.51 = (bf16[4,128,256]{2,1,0:T(8,128)(2,1)S(1)}, bf16[4,128,256]{2,1,0:T(8,128)(2,1)S(1)}) custom-call(s32[8,8]{1,0:T(8,128)S(1)} %get-tuple-element.33.refs_0_, bf16[256,128,128]{2,1,0:T(8,128)(2,1)S(1)} %bitcast.20, bf16[8,128,256]{2,1,0:T(8,128)(2,1)S(1)} %pad_maximum_fusion.refs_2_, bf16[8,128,256]{2,1,0:T(8,128)(2,1)S(1)} %collective-permute-done.7.refs_3_), custom_call_target="tpu_custom_call" | custom-call | tf_op jit(solution)/shard_map/pallas_call | solution.py:51
  34.6 1.6 %collective-permute-start.12 = (bf16[4,128,256]{2,1,0:T(8,128)(2,1)S(1)}, bf16[4,128,256]{2,1,0:T(8,128)(2,1)S(1)}, u32[]{:S(2)}, u32[]{:S(2)}) collective-permute-start(bf16[4,128,256]{2,1,0:T(8,128)(2,1)S(1)} %get-tuple-element.28), channel_id=1, source_target_pairs={{0,8},{4,12},{8,0},{12,4},{1,9},{5,13},{9,1},{13,5},{2,10},{6,14},... | collective-permute-start | bytes 786440 | tf_op jit(solution)/shard_map/ppermute | solution.py:62
  36.7 2.2 %shard_map.50 = (bf16[4,128,256]{2,1,0:T(8,128)(2,1)S(1)}, f32[4,128,256]{2,1,0:T(8,128)S(1)}, f32[4,128,256]{2,1,0:T(8,128)S(1)}, bf16[4,128,256]{2,1,0:T(8,128)(2,1)S(1)}) custom-call(s32[16,8]{1,0:T(8,128)S(1)} %slice.43.refs_0_, bf16[256,128,128]{2,1,0:T(8,128)(2,1)S(1)} %bitcast.21, bf16[8,128,256]{2,1,0:T(8,128)(2,1)S(1)} %pad_maximum_fusion.refs_2_, ...), custom_call_target="tpu_custom_call" | custom-call | tf_op jit(solution)/shard_map/pallas_call | solution.py:51
  39.4 1.7 %collective-permute-start.8 = (bf16[4,128,256]{2,1,0:T(8,128)(2,1)S(1)}, bf16[4,128,256]{2,1,0:T(8,128)(2,1)S(1)}, u32[]{:S(2)}, u32[]{:S(2)}) collective-permute-start(bf16[4,128,256]{2,1,0:T(8,128)(2,1)S(1)} %get-tuple-element.23), channel_id=1, source_target_pairs={{0,4},{4,0},{8,12},{12,8},{1,5},{5,1},{9,13},{13,9},{2,6},{6,2},{1... | collective-permute-start | bytes 786440 | tf_op jit(solution)/shard_map/ppermute | solution.py:62
  41.1 2.8 %collective-permute-done.12 = bf16[4,128,256]{2,1,0:T(8,128)(2,1)S(1)} collective-permute-done((bf16[4,128,256]{2,1,0:T(8,128)(2,1)S(1)}, bf16[4,128,256]{2,1,0:T(8,128)(2,1)S(1)}, u32[]{:S(2)}, u32[]{:S(2)}) %collective-permute-start.12) | collective-permute-done | bytes 262176 | tf_op jit(solution)/shard_map/ppermute | solution.py:62
  44.1 1.3 %collective-permute-done.9 = bf16[4,128,256]{2,1,0:T(8,128)(2,1)S(1)} collective-permute-done((bf16[4,128,256]{2,1,0:T(8,128)(2,1)S(1)}, bf16[4,128,256]{2,1,0:T(8,128)(2,1)S(1)}, u32[]{:S(2)}, u32[]{:S(2)}) %collective-permute-start.9) | collective-permute-done | bytes 262176 | tf_op jit(solution)/shard_map/ppermute | solution.py:62
  46.2 1.7 %shard_map.49 = f32[8,128,256]{2,1,0:T(8,128)S(1)} custom-call(s32[8,8]{1,0:T(8,128)S(1)} %get-tuple-element.34.refs_0_, bf16[256,128,128]{2,1,0:T(8,128)(2,1)S(1)} %bitcast.22, bf16[8,128,256]{2,1,0:T(8,128)(2,1)S(1)} %pad_maximum_fusion.refs_2_, bf16[8,128,256]{2,1,0:T(8,128)(2,1)S(1)} %collective-permute-done.7.refs_3_), custom_call_target="tpu_custom_call" | custom-call | tf_op jit(solution)/shard_map/pallas_call | solution.py:51
  47.8 1.6 %collective-permute-done.11 = bf16[4,128,256]{2,1,0:T(8,128)(2,1)S(1)} collective-permute-done((bf16[4,128,256]{2,1,0:T(8,128)(2,1)S(1)}, bf16[4,128,256]{2,1,0:T(8,128)(2,1)S(1)}, u32[]{:S(2)}, u32[]{:S(2)}) %collective-permute-start.11) | collective-permute-done | bytes 262176 | tf_op jit(solution)/shard_map/ppermute | solution.py:62
  49.5 1.6 %collective-permute-done.8 = bf16[4,128,256]{2,1,0:T(8,128)(2,1)S(1)} collective-permute-done((bf16[4,128,256]{2,1,0:T(8,128)(2,1)S(1)}, bf16[4,128,256]{2,1,0:T(8,128)(2,1)S(1)}, u32[]{:S(2)}, u32[]{:S(2)}) %collective-permute-start.8) | collective-permute-done | bytes 262176 | tf_op jit(solution)/shard_map/ppermute | solution.py:62
  51.0 4.5 %collective-permute-done.13 = bf16[4,128,256]{2,1,0:T(8,128)(2,1)S(1)} collective-permute-done((bf16[4,128,256]{2,1,0:T(8,128)(2,1)S(1)}, bf16[4,128,256]{2,1,0:T(8,128)(2,1)S(1)}, u32[]{:S(2)}, u32[]{:S(2)}) %collective-permute-start.13) | collective-permute-done | bytes 262176 | tf_op jit(solution)/shard_map/ppermute | solution.py:62
  55.7 0.8 %pad_maximum_fusion.1 = bf16[8,128,256]{2,1,0:T(8,128)(2,1)} fusion(bf16[4,128,256]{2,1,0:T(8,128)(2,1)S(1)} %get-tuple-element.30, bf16[4,128,256]{2,1,0:T(8,128)(2,1)S(1)} %get-tuple-element.29), kind=kLoop, calls=%fused_computation.13 | loop fusion | flops 262144 | bytes 1048576 | tf_op jit(solution)/shard_map/concatenate | solution.py:102
  (38 shorter events, 5.7 us)
Async XLA Ops:
  0.0 2.8 %collective-permute-start = (bf16[8,128,256]{2,1,0:T(8,128)(2,1)}, bf16[8,128,256]{2,1,0:T(8,128)(2,1)S(1)}, u32[]{:S(2)}, u32[]{:S(2)}) collective-permute-start(bf16[8,128,256]{2,1,0:T(8,128)(2,1)} %bitcast.23), channel_id=1, source_target_pairs={{0,16},{16,0},{1,17},{17,1},{2,18},{18,2},{3,19},{19,3},{4,20},{20... | collective-permute-start | bytes 1572872 | tf_op jit(solution)/shard_map/ppermute | solution.py:88
  2.8 3.4 %copy-start = (bf16[1,1,256,128,128]{4,3,2,1,0:T(8,128)(2,1)S(1)}, bf16[1,1,256,128,128]{4,3,2,1,0:T(8,128)(2,1)}, u32[]{:S(2)}) copy-start(bf16[1,1,256,128,128]{4,3,2,1,0:T(8,128)(2,1)} %param.5) | copy-start | bytes 25165828
  6.2 1.0 %copy-start.1 = (bf16[1024,256]{1,0:T(8,128)(2,1)S(1)}, bf16[1024,256]{1,0:T(8,128)(2,1)}, u32[]{:S(2)}) copy-start(bf16[1024,256]{1,0:T(8,128)(2,1)} %param.4) | copy-start | bytes 1572868
  7.2 14.9 %slice-start = ((s8[8388608]{0:T(1024)(128)(4,1)}), s8[4194304]{0:T(1024)(128)(4,1)S(1)}, s32[]{:S(2)}) async-start(s8[8388608]{0:T(1024)(128)(4,1)} %bitcast.17), calls=%async_computation | async-start | bytes 8388608
  8.6 9.7 %collective-permute-start.2 = (bf16[4,128,256]{2,1,0:T(8,128)(2,1)S(1)}, bf16[4,128,256]{2,1,0:T(8,128)(2,1)S(1)}, u32[]{:S(2)}, u32[]{:S(2)}) collective-permute-start(bf16[4,128,256]{2,1,0:T(8,128)(2,1)S(1)} %get-tuple-element.19), channel_id=1, source_target_pairs={{0,4},{4,0},{8,12},{12,8},{1,5},{5,1},{9,13},{13,9},{2,6},{6,2},{1... | collective-permute-start | bytes 786440 | tf_op jit(solution)/shard_map/ppermute | solution.py:62
  11.2 9.3 %collective-permute-start.5 = (bf16[4,128,256]{2,1,0:T(8,128)(2,1)S(1)}, bf16[4,128,256]{2,1,0:T(8,128)(2,1)S(1)}, u32[]{:S(2)}, u32[]{:S(2)}) collective-permute-start(bf16[4,128,256]{2,1,0:T(8,128)(2,1)S(1)} %get-tuple-element.22), channel_id=1, source_target_pairs={{0,8},{4,12},{8,0},{12,4},{1,9},{5,13},{9,1},{13,5},{2,10},{6,14},... | collective-permute-start | bytes 786440 | tf_op jit(solution)/shard_map/ppermute | solution.py:62
  12.7 9.4 %slice-start.1 = ((s8[8388608]{0:T(1024)(128)(4,1)}), s8[4194304]{0:T(1024)(128)(4,1)S(1)}, s32[]{:S(2)}) async-start(s8[8388608]{0:T(1024)(128)(4,1)} %bitcast.17), calls=%async_computation.1 | async-start | bytes 8388608
  14.8 9.3 %collective-permute-start.1 = (bf16[4,128,256]{2,1,0:T(8,128)(2,1)S(1)}, bf16[4,128,256]{2,1,0:T(8,128)(2,1)S(1)}, u32[]{:S(2)}, u32[]{:S(2)}) collective-permute-start(bf16[4,128,256]{2,1,0:T(8,128)(2,1)S(1)} %get-tuple-element.17), channel_id=1, source_target_pairs={{0,4},{4,0},{8,12},{12,8},{1,5},{5,1},{9,13},{13,9},{2,6},{6,2},{1... | collective-permute-start | bytes 786440 | tf_op jit(solution)/shard_map/ppermute | solution.py:62
  15.4 10.6 %collective-permute-start.4 = (bf16[4,128,256]{2,1,0:T(8,128)(2,1)S(1)}, bf16[4,128,256]{2,1,0:T(8,128)(2,1)S(1)}, u32[]{:S(2)}, u32[]{:S(2)}) collective-permute-start(bf16[4,128,256]{2,1,0:T(8,128)(2,1)S(1)} %get-tuple-element.20), channel_id=1, source_target_pairs={{0,8},{4,12},{8,0},{12,4},{1,9},{5,13},{9,1},{13,5},{2,10},{6,14},... | collective-permute-start | bytes 786440 | tf_op jit(solution)/shard_map/ppermute | solution.py:62
  18.4 12.4 %collective-permute-start.3 = (bf16[4,128,256]{2,1,0:T(8,128)(2,1)S(1)}, bf16[4,128,256]{2,1,0:T(8,128)(2,1)S(1)}, u32[]{:S(2)}, u32[]{:S(2)}) collective-permute-start(bf16[4,128,256]{2,1,0:T(8,128)(2,1)S(1)} %add_convert_fusion.3), channel_id=1, source_target_pairs={{0,8},{4,12},{8,0},{12,4},{1,9},{5,13},{9,1},{13,5},{2,10},{6,14},... | collective-permute-start | bytes 786440 | tf_op jit(solution)/shard_map/ppermute | solution.py:62
  20.6 10.3 %collective-permute-start.6 = (bf16[4,128,256]{2,1,0:T(8,128)(2,1)S(1)}, bf16[4,128,256]{2,1,0:T(8,128)(2,1)S(1)}, u32[]{:S(2)}, u32[]{:S(2)}) collective-permute-start(bf16[4,128,256]{2,1,0:T(8,128)(2,1)S(1)} %add_convert_fusion.2), channel_id=1, source_target_pairs={{0,4},{4,0},{8,12},{12,8},{1,5},{5,1},{9,13},{13,9},{2,6},{6,2},{1... | collective-permute-start | bytes 786440 | tf_op jit(solution)/shard_map/ppermute | solution.py:62
  31.1 2.0 %collective-permute-start.7 = (bf16[8,128,256]{2,1,0:T(8,128)(2,1)S(1)}, bf16[8,128,256]{2,1,0:T(8,128)(2,1)S(1)}, u32[]{:S(2)}, u32[]{:S(2)}) collective-permute-start(bf16[8,128,256]{2,1,0:T(8,128)(2,1)S(1)} %pad_maximum_fusion.refs_2_), channel_id=1, source_target_pairs={{0,16},{16,0},{1,17},{17,1},{2,18},{18,2},{3,19},{19,3},{4,20},{20... | collective-permute-start | bytes 1572872 | tf_op jit(solution)/shard_map/ppermute | solution.py:88
  34.6 9.2 %collective-permute-start.12 = (bf16[4,128,256]{2,1,0:T(8,128)(2,1)S(1)}, bf16[4,128,256]{2,1,0:T(8,128)(2,1)S(1)}, u32[]{:S(2)}, u32[]{:S(2)}) collective-permute-start(bf16[4,128,256]{2,1,0:T(8,128)(2,1)S(1)} %get-tuple-element.28), channel_id=1, source_target_pairs={{0,8},{4,12},{8,0},{12,4},{1,9},{5,13},{9,1},{13,5},{2,10},{6,14},... | collective-permute-start | bytes 786440 | tf_op jit(solution)/shard_map/ppermute | solution.py:62
  36.2 9.2 %collective-permute-start.9 = (bf16[4,128,256]{2,1,0:T(8,128)(2,1)S(1)}, bf16[4,128,256]{2,1,0:T(8,128)(2,1)S(1)}, u32[]{:S(2)}, u32[]{:S(2)}) collective-permute-start(bf16[4,128,256]{2,1,0:T(8,128)(2,1)S(1)} %get-tuple-element.25), channel_id=1, source_target_pairs={{0,4},{4,0},{8,12},{12,8},{1,5},{5,1},{9,13},{13,9},{2,6},{6,2},{1... | collective-permute-start | bytes 786440 | tf_op jit(solution)/shard_map/ppermute | solution.py:62
  39.0 10.5 %collective-permute-start.11 = (bf16[4,128,256]{2,1,0:T(8,128)(2,1)S(1)}, bf16[4,128,256]{2,1,0:T(8,128)(2,1)S(1)}, u32[]{:S(2)}, u32[]{:S(2)}) collective-permute-start(bf16[4,128,256]{2,1,0:T(8,128)(2,1)S(1)} %get-tuple-element.26), channel_id=1, source_target_pairs={{0,8},{4,12},{8,0},{12,4},{1,9},{5,13},{9,1},{13,5},{2,10},{6,14},... | collective-permute-start | bytes 786440 | tf_op jit(solution)/shard_map/ppermute | solution.py:62
  39.4 11.6 %collective-permute-start.8 = (bf16[4,128,256]{2,1,0:T(8,128)(2,1)S(1)}, bf16[4,128,256]{2,1,0:T(8,128)(2,1)S(1)}, u32[]{:S(2)}, u32[]{:S(2)}) collective-permute-start(bf16[4,128,256]{2,1,0:T(8,128)(2,1)S(1)} %get-tuple-element.23), channel_id=1, source_target_pairs={{0,4},{4,0},{8,12},{12,8},{1,5},{5,1},{9,13},{13,9},{2,6},{6,2},{1... | collective-permute-start | bytes 786440 | tf_op jit(solution)/shard_map/ppermute | solution.py:62
  43.9 11.6 %collective-permute-start.13 = (bf16[4,128,256]{2,1,0:T(8,128)(2,1)S(1)}, bf16[4,128,256]{2,1,0:T(8,128)(2,1)S(1)}, u32[]{:S(2)}, u32[]{:S(2)}) collective-permute-start(bf16[4,128,256]{2,1,0:T(8,128)(2,1)S(1)} %add_convert_fusion), channel_id=1, source_target_pairs={{0,4},{4,0},{8,12},{12,8},{1,5},{5,1},{9,13},{13,9},{2,6},{6,2},{1... | collective-permute-start | bytes 786440 | tf_op jit(solution)/shard_map/ppermute | solution.py:62
  45.5 10.0 %collective-permute-start.10 = (bf16[4,128,256]{2,1,0:T(8,128)(2,1)S(1)}, bf16[4,128,256]{2,1,0:T(8,128)(2,1)S(1)}, u32[]{:S(2)}, u32[]{:S(2)}) collective-permute-start(bf16[4,128,256]{2,1,0:T(8,128)(2,1)S(1)} %add_convert_fusion.1), channel_id=1, source_target_pairs={{0,8},{4,12},{8,0},{12,4},{1,9},{5,13},{9,1},{13,5},{2,10},{6,14},... | collective-permute-start | bytes 786440 | tf_op jit(solution)/shard_map/ppermute | solution.py:62

commit v2 on v1

v2 whole, which is shorter than its diff:
```python
import functools

import jax
import jax.numpy as jnp
from jax import lax
from jax.experimental import pallas as pl
from jax.experimental.pallas import tpu as pltpu
from jax.sharding import PartitionSpec as P

TILE_SIZE = 128
BLOCK_ROWS = 32
COL_SHIFT = 16
CHUNK = 128
LOADS = 4

VMEM = pl.BlockSpec(memory_space=pltpu.VMEM)
SMEM = pl.BlockSpec(memory_space=pltpu.SMEM)
HBM = pl.BlockSpec(memory_space=pltpu.HBM)


def directions():
    core = lax.axis_index("row") % 2
    return 1 + core, 2 - core


def load_kernel(own_first, share, blocks, index, count, tiles, table, tiles_here, index_here, count_here, rows, sem):
    slots = tiles.shape[0]
    part = slots // LOADS
    small = [
        pltpu.make_async_copy(index, index_here.at[0:2], sem.at[LOADS]),
        pltpu.make_async_copy(count, count_here, sem.at[LOADS + 1]),
    ]
    copies = [
        pltpu.make_async_copy(
            tiles.at[pl.ds(i * part, part)], tiles_here.at[pl.ds(i * part, part)], sem.at[i]
        )
        for i in range(LOADS)
    ]
    for copy in small + copies:
        copy.start()
    lane = lax.broadcasted_iota(jnp.int32, (BLOCK_ROWS, TILE_SIZE), 1)
    quarter = lane // share
    first, second = directions()
    flip = jnp.where(quarter == 0, 3, jnp.where(quarter == 1, first, jnp.where(quarter == 2, second, 0)))
    wanted = (lax.axis_index("col") ^ flip) * share + lane % share
    slot = lax.broadcasted_iota(jnp.int32, (BLOCK_ROWS, 1), 0)
    for copy in small:
        copy.wait()
    by_slot = index_here[...].T
    for level in range(slots // BLOCK_ROWS):
        here = by_slot[level * BLOCK_ROWS : (level + 1) * BLOCK_ROWS]
        row, block = here[:, 0:1], here[:, 1:2]
        if own_first:
            block = block ^ (lax.axis_index("row") * share)
        block = jnp.where(level * BLOCK_ROWS < count_here[0, 0], block, blocks)
        entry = ((slot + level * BLOCK_ROWS) << COL_SHIFT) | block
        rows[level : level + 1] = jnp.sum(jnp.where(row == wanted, entry, 0), axis=0, keepdims=True)
    to_scalar = pltpu.make_async_copy(rows, table, sem.at[LOADS])
    to_scalar.start()
    to_scalar.wait()
    for copy in copies:
        copy.wait()


def load(tile_index, tile_count, tiles, own_first, share, blocks):
    slots = tiles.shape[0]
    levels = slots // BLOCK_ROWS
    return pl.pallas_call(
        functools.partial(load_kernel, own_first, share, blocks),
        out_shape=[pltpu.SMEM((levels, TILE_SIZE), jnp.int32), pltpu.VMEM(tiles.shape, tiles.dtype)],
        in_specs=[HBM, HBM, HBM],
        out_specs=[SMEM, VMEM],
        scratch_shapes=[
            pltpu.VMEM((8, slots), jnp.int32),
            pltpu.SMEM((1, 1), jnp.int32),
            pltpu.VMEM((levels, TILE_SIZE), jnp.int32),
            pltpu.SemaphoreType.DMA((LOADS + 2,)),
        ],
        compiler_params=pltpu.CompilerParams(vmem_limit_bytes=50 << 20),
    )(tile_index, tile_count, tiles)


def sweep_kernel(counts, first, sources, *refs):
    table, tiles = refs[:2]
    source_refs = refs[2 : 2 + sources]
    out_refs = refs[2 + sources : -1]
    panel = refs[-1]
    at = 0
    for source in source_refs:
        panel[at : at + source.shape[0]] = source[...]
        at += source.shape[0]
    panel[at] = jnp.zeros_like(panel[at])
    levels = table.shape[0]
    split = panel.shape[2] // CHUNK
    for i, count in enumerate(counts):
        outs = out_refs[i * split : (i + 1) * split]

        def row(b, carry, outs=outs, first=first):
            left, right = [], []
            for k in range(levels):
                entry = table[k, first + b]
                left.append(tiles[entry >> COL_SHIFT])
                right.append(panel[entry & ((1 << COL_SHIFT) - 1)])
            total = jnp.dot(
                jnp.concatenate(left, 1), jnp.concatenate(right, 0), preferred_element_type=jnp.float32
            )
            for j, out in enumerate(outs):
                out[b] = total[:, j * CHUNK : (j + 1) * CHUNK].astype(out.dtype)
            return carry

        lax.fori_loop(0, count, row, 0, unroll=4)
        first += count


def sweep(table, tiles, sources, first, outs):
    blocks = sum(s.shape[0] for s in sources)
    columns = sources[0].shape[2]
    split = columns // CHUNK
    rows, depth = sum(n for n, _ in outs), table.shape[0] * TILE_SIZE
    out = pl.pallas_call(
        functools.partial(sweep_kernel, [n for n, _ in outs], first, len(sources)),
        out_shape=[
            jax.ShapeDtypeStruct((n, TILE_SIZE, CHUNK), dtype) for n, dtype in outs for _ in range(split)
        ],
        in_specs=[SMEM] + [VMEM] * (1 + len(sources)),
        out_specs=[VMEM] * (len(outs) * split),
        scratch_shapes=[pltpu.VMEM((blocks + 1, TILE_SIZE, columns), jnp.bfloat16)],
        compiler_params=pltpu.CompilerParams(vmem_limit_bytes=12 << 20),
        cost_estimate=pl.CostEstimate(
            flops=2 * rows * TILE_SIZE * depth * columns * 2,
            transcendentals=0,
            bytes_accessed=rows * TILE_SIZE * (depth + columns) * 2,
        ),
    )(table, tiles, *sources)
    return [out[i * split : (i + 1) * split] for i in range(len(outs))]


def exchange(values, second, n_row, n_col):
    pairs = []
    for r in range(n_row):
        flip = 1 + r % 2
        if second:
            flip = 3 - flip
        pairs += [(r * n_col + c, r * n_col + (c ^ flip)) for c in range(n_col)]
    return lax.ppermute(values, ("row", "col"), pairs)


def panel_of(blocks, n_row):
    if n_row == 2:
        return [blocks, lax.ppermute(blocks, "row", [(0, 1), (1, 0)])]
    return [lax.all_gather(blocks, "row", axis=0, tiled=True)]


def local(n_row, n_col, source_columns, tiles, tile_index, tile_count):
    f32, bf16 = jnp.float32, jnp.bfloat16
    share = BLOCK_ROWS // n_col
    columns = source_columns.shape[1]
    split = columns // CHUNK
    blocks = n_row * share
    whole = panel_of(source_columns.reshape(share, TILE_SIZE, columns), n_row)
    table, tiles = load(
        tile_index.reshape(-1, 2).T, tile_count, tiles.reshape(-1, TILE_SIZE, TILE_SIZE), n_row == 2, share, blocks
    )

    first = functools.partial(exchange, second=False, n_row=n_row, n_col=n_col)
    second = functools.partial(exchange, second=True, n_row=n_row, n_col=n_col)

    def couple(source):
        (far,) = sweep(table, tiles, source, 0, [(share, bf16)])
        far = [first(f) for f in far]
        near, kept = sweep(table, tiles, source, share, [(share, bf16), (share, f32)])
        near = [first(n) for n in near]
        (own,) = sweep(table, tiles, source, 3 * share, [(share, f32)])
        last = [second((k + f.astype(f32)).astype(bf16)) for k, f in zip(kept, far)]
        return [(o + n.astype(f32) + t.astype(f32)).astype(bf16) for o, n, t in zip(own, near, last)]

    once = couple(whole)
    twice = [couple(panel_of(o, n_row))[0] for o in once]
    return jnp.concatenate(twice, -1).reshape(source_columns.shape)


def solution(mesh):
    n_row, n_col = mesh.shape["row"], mesh.shape["col"]
    assert n_col == 4
    placed = (
        P(("mem", "row", "col"), None),
        P(("mem", "row"), "col", None, None, None),
        P(("mem", "row"), "col", None, None),
        P(("mem", "row"), "col"),
    )
    return jax.shard_map(
        functools.partial(local, n_row, n_col),
        mesh=mesh,
        in_specs=placed,
        out_specs=P(("mem", "row", "col"), None),
        check_vma=False,
    )
```

time: 56.8 us -> 49.8 us (0.88)
  waiting for transfers between devices: 23.6 us -> 15 us
  local copies, waits for them, and re-layouts: 5.19 us -> 0.01 us
  Pallas kernels: 10.6 us -> 14.4 us
  starting transfers between devices: 13.9 us -> 17.7 us
  other arithmetic: 2.44 us -> 1.46 us
    ppermute x14 -> x15, waiting for transfers between devices: 23.6 us -> 15 us  [the longest x12 15 us: exchange(): return lax.ppermute(values, ('row', 'col'), pairs)]
    unnamed x8 -> x2, local copies, waits for them, and re-layouts: 4.43 us -> 0.01 us
    pallas_call x6 -> x10, Pallas kernels: 10.6 us -> 14.4 us  [the longest x9 10.9 us: sweep(): pl.pallas_call(functools.partial(sweep_kernel, [n for n, _ in outs], firs...]
    ppermute x14 -> x15, starting transfers between devices: 13.9 us -> 17.7 us  [the longest x12 17.1 us: exchange(): return lax.ppermute(values, ('row', 'col'), pairs)]
    reshape x1 -> x0, local copies, waits for them, and re-layouts: 0.76 us -> none  [row_table(): index = tile_index.reshape(-1, BLOCK_ROWS, 2)]
    reduce_sum x1 -> x0, other arithmetic: 0.69 us -> none  [row_table(): return jnp.sum(jnp.where(hit, entry[None], 0), axis=-1, dtype=jnp.int32)]
  transfers between devices with their start and end apart: 14 -> 15, of which waited for: 10 -> 9; matrix products, arithmetic and copies ran while one was open for 3% -> 1% of each run, Pallas kernels for 13% -> 27%
where the time goes in v2:
time: 49.8 us; the launch traced here: 49.5 us
  starting transfers between devices  17.7 us (36%)
  waiting for transfers between devices  15 us (30%)
  Pallas kernels  14.4 us (29%)
  other arithmetic  1.46 us (3%)
  between operations  0.83 us (2%)
    ppermute x12, starting transfers between devices, exchange(): return lax.ppermute(values, ('row', 'col'), pairs)  17.1 us
    ppermute x12, waiting for transfers between devices, exchange(): return lax.ppermute(values, ('row', 'col'), pairs)  15 us
    pallas_call x9, Pallas kernels, sweep(): pl.pallas_call(functools.partial(sweep_kernel, [n for n, _ in outs], firs...  10.9 us
    pallas_call x1, Pallas kernels, load(): pl.pallas_call(functools.partial(load_kernel, own_first, share, blocks),...  3.53 us
  transfers between devices with their start and end apart: 15, of which 9 were waited for; matrix products, arithmetic and copies ran while one was open for 1% of the time, Pallas kernels for 27%

profile of v2, /device:TPU:0, one launch (start us, length us, event | category | flops | bytes accessed | tf_op | source)
XLA Modules:
  0.0 49.5 jit_solution(14088487291749033247)
XLA Ops:
  1.1 3.5 %shard_map.46 = (s32[8,128]{1,0:T(8,128)S(4)}, bf16[256,128,128]{2,1,0:T(8,128)(2,1)S(1)}) custom-call(s32[2,256]{1,0:T(2,128)} %bitcast.11, s32[1,1]{1,0:T(1,128)S(6)} %copy.5.count, bf16[256,128,128]{2,1,0:T(8,128)(2,1)} %bitcast.10), custom_call_target="tpu_custom_call" | custom-call | tf_op jit(solution)/shard_map/pallas_call | solution.py:68
  4.7 1.0 %shard_map.49 = (bf16[8,128,128]{2,1,0:T(8,128)(2,1)S(1)}, bf16[8,128,128]{2,1,0:T(8,128)(2,1)S(1)}) custom-call(s32[8,128]{1,0:T(8,128)S(4)} %get-tuple-element.19.refs_0_, bf16[256,128,128]{2,1,0:T(8,128)(2,1)S(1)} %get-tuple-element.20.refs_1_, bf16[8,128,256]{2,1,0:T(8,128)(2,1)S(1)} %bitcast.7, bf16[8,128,256]{2,1,0:T(8,128)(2,1)S(1)} %collective-permute-done.refs_3_), custom_call_target="tpu_custom_call" | custom-call | flops 1073741824 | bytes 2621440 | tf_op jit(solution)/shard_map/pallas_call | solution.py:120
  5.7 2.6 %collective-permute-start.9 = (bf16[8,128,128]{2,1,0:T(8,128)(2,1)S(1)}, bf16[8,128,128]{2,1,0:T(8,128)(2,1)S(1)}, u32[]{:S(2)}, u32[]{:S(2)}) collective-permute-start(bf16[8,128,128]{2,1,0:T(8,128)(2,1)S(1)} %get-tuple-element.30), channel_id=1, source_target_pairs={{0,4},{4,0},{8,12},{12,8},{16,24},{20,28},{24,16},{28,20},{1,5},{5... | collective-permute-start | bytes 786440 | tf_op jit(solution)/shard_map/ppermute | solution.py:145
  8.4 1.9 %shard_map.48 = (bf16[8,128,128]{2,1,0:T(8,128)(2,1)S(1)}, bf16[8,128,128]{2,1,0:T(8,128)(2,1)S(1)}, f32[8,128,128]{2,1,0:T(8,128)S(1)}, f32[8,128,128]{2,1,0:T(8,128)S(1)}) custom-call(s32[8,128]{1,0:T(8,128)S(4)} %get-tuple-element.19.refs_0_, bf16[256,128,128]{2,1,0:T(8,128)(2,1)S(1)} %get-tuple-element.20.refs_1_, bf16[8,128,256]{2,1,0:T(8,128)(2,1)S(1)} %bitcast.8, ...), custom_call_target="tpu_custom_call" | custom-call | flops 2147483648 | bytes 5242880 | tf_op jit(solution)/shard_map/pallas_call | solution.py:120
  10.2 2.0 %collective-permute-start.8 = (bf16[8,128,128]{2,1,0:T(8,128)(2,1)S(1)}, bf16[8,128,128]{2,1,0:T(8,128)(2,1)S(1)}, u32[]{:S(2)}, u32[]{:S(2)}) collective-permute-start(bf16[8,128,128]{2,1,0:T(8,128)(2,1)S(1)} %get-tuple-element.28), channel_id=1, source_target_pairs={{0,4},{4,0},{8,12},{12,8},{16,24},{20,28},{24,16},{28,20},{1,5},{5... | collective-permute-start | bytes 786440 | tf_op jit(solution)/shard_map/ppermute | solution.py:145
  12.7 2.1 %collective-permute-start.10 = (bf16[8,128,128]{2,1,0:T(8,128)(2,1)S(1)}, bf16[8,128,128]{2,1,0:T(8,128)(2,1)S(1)}, u32[]{:S(2)}, u32[]{:S(2)}) collective-permute-start(bf16[8,128,128]{2,1,0:T(8,128)(2,1)S(1)} %add_convert_fusion.3), channel_id=1, source_target_pairs={{0,8},{4,12},{8,0},{12,4},{16,20},{20,16},{24,28},{28,24},{1,9},{5... | collective-permute-start | bytes 786440 | tf_op jit(solution)/shard_map/ppermute | solution.py:145
  15.6 2.4 %collective-permute-start.3 = (bf16[8,128,128]{2,1,0:T(8,128)(2,1)S(1)}, bf16[8,128,128]{2,1,0:T(8,128)(2,1)S(1)}, u32[]{:S(2)}, u32[]{:S(2)}) collective-permute-start(bf16[8,128,128]{2,1,0:T(8,128)(2,1)S(1)} %add_convert_fusion.7), channel_id=1, source_target_pairs={{0,8},{4,12},{8,0},{12,4},{16,20},{20,16},{24,28},{28,24},{1,9},{5... | collective-permute-start | bytes 786440 | tf_op jit(solution)/shard_map/ppermute | solution.py:145
  18.0 1.0 %shard_map.47 = (f32[8,128,128]{2,1,0:T(8,128)S(1)}, f32[8,128,128]{2,1,0:T(8,128)S(1)}) custom-call(s32[8,128]{1,0:T(8,128)S(4)} %get-tuple-element.19.refs_0_, bf16[256,128,128]{2,1,0:T(8,128)(2,1)S(1)} %get-tuple-element.20.refs_1_, bf16[8,128,256]{2,1,0:T(8,128)(2,1)S(1)} %bitcast.9, bf16[8,128,256]{2,1,0:T(8,128)(2,1)S(1)} %collective-permute-done.refs_3_), custom_call_target="tpu_custom_call" | custom-call | flops 1073741824 | bytes 2621440 | tf_op jit(solution)/shard_map/pallas_call | solution.py:120
  19.0 2.1 %collective-permute-done.8 = bf16[8,128,128]{2,1,0:T(8,128)(2,1)S(1)} collective-permute-done((bf16[8,128,128]{2,1,0:T(8,128)(2,1)S(1)}, bf16[8,128,128]{2,1,0:T(8,128)(2,1)S(1)}, u32[]{:S(2)}, u32[]{:S(2)}) %collective-permute-start.8) | collective-permute-done | bytes 262176 | tf_op jit(solution)/shard_map/ppermute | solution.py:145
  22.2 4.5 %collective-permute-done.1 = bf16[8,128,128]{2,1,0:T(8,128)(2,1)S(1)} collective-permute-done((bf16[8,128,128]{2,1,0:T(8,128)(2,1)S(1)}, bf16[8,128,128]{2,1,0:T(8,128)(2,1)S(1)}, u32[]{:S(2)}, u32[]{:S(2)}) %collective-permute-start.1) | collective-permute-done | bytes 262176 | tf_op jit(solution)/shard_map/ppermute | solution.py:145
  26.9 0.9 %shard_map.55 = bf16[8,128,128]{2,1,0:T(8,128)(2,1)S(1)} custom-call(s32[8,128]{1,0:T(8,128)S(4)} %get-tuple-element.19.refs_0_, bf16[256,128,128]{2,1,0:T(8,128)(2,1)S(1)} %get-tuple-element.20.refs_1_, bf16[8,128,128]{2,1,0:T(8,128)(2,1)S(1)} %add_convert_fusion.2.refs_2_, bf16[8,128,128]{2,1,0:T(8,128)(2,1)S(1)} %collective-permute-done.11.refs_3_), custom_call_target="tpu_custom_call" | custom-call | flops 536870912 | bytes 2359296 | tf_op jit(solution)/shard_map/pallas_call | solution.py:120
  27.8 2.1 %collective-permute-start.13 = (bf16[8,128,128]{2,1,0:T(8,128)(2,1)S(1)}, bf16[8,128,128]{2,1,0:T(8,128)(2,1)S(1)}, u32[]{:S(2)}, u32[]{:S(2)}) collective-permute-start(bf16[8,128,128]{2,1,0:T(8,128)(2,1)S(1)} %shard_map.55), channel_id=1, source_target_pairs={{0,4},{4,0},{8,12},{12,8},{16,24},{20,28},{24,16},{28,20},{1,5},{5... | collective-permute-start | bytes 786440 | tf_op jit(solution)/shard_map/ppermute | solution.py:145
  29.8 1.7 %shard_map.54 = (bf16[8,128,128]{2,1,0:T(8,128)(2,1)S(1)}, f32[8,128,128]{2,1,0:T(8,128)S(1)}) custom-call(s32[8,128]{1,0:T(8,128)S(4)} %get-tuple-element.19.refs_0_, bf16[256,128,128]{2,1,0:T(8,128)(2,1)S(1)} %get-tuple-element.20.refs_1_, bf16[8,128,128]{2,1,0:T(8,128)(2,1)S(1)} %add_convert_fusion.2.refs_2_, ...), custom_call_target="tpu_custom_call" | custom-call | flops 1073741824 | bytes 4718592 | tf_op jit(solution)/shard_map/pallas_call | solution.py:120
  31.7 0.9 %shard_map.52 = bf16[8,128,128]{2,1,0:T(8,128)(2,1)S(1)} custom-call(s32[8,128]{1,0:T(8,128)S(4)} %get-tuple-element.19.refs_0_, bf16[256,128,128]{2,1,0:T(8,128)(2,1)S(1)} %get-tuple-element.20.refs_1_, bf16[8,128,128]{2,1,0:T(8,128)(2,1)S(1)} %add_convert_fusion.6.refs_2_, bf16[8,128,128]{2,1,0:T(8,128)(2,1)S(1)} %collective-permute-done.4.refs_3_), custom_call_target="tpu_custom_call" | custom-call | flops 536870912 | bytes 2359296 | tf_op jit(solution)/shard_map/pallas_call | solution.py:120
  32.6 2.1 %collective-permute-start.6 = (bf16[8,128,128]{2,1,0:T(8,128)(2,1)S(1)}, bf16[8,128,128]{2,1,0:T(8,128)(2,1)S(1)}, u32[]{:S(2)}, u32[]{:S(2)}) collective-permute-start(bf16[8,128,128]{2,1,0:T(8,128)(2,1)S(1)} %shard_map.52), channel_id=1, source_target_pairs={{0,4},{4,0},{8,12},{12,8},{16,24},{20,28},{24,16},{28,20},{1,5},{5... | collective-permute-start | bytes 786440 | tf_op jit(solution)/shard_map/ppermute | solution.py:145
  34.7 1.7 %shard_map.51 = (bf16[8,128,128]{2,1,0:T(8,128)(2,1)S(1)}, f32[8,128,128]{2,1,0:T(8,128)S(1)}) custom-call(s32[8,128]{1,0:T(8,128)S(4)} %get-tuple-element.19.refs_0_, bf16[256,128,128]{2,1,0:T(8,128)(2,1)S(1)} %get-tuple-element.20.refs_1_, bf16[8,128,128]{2,1,0:T(8,128)(2,1)S(1)} %add_convert_fusion.6.refs_2_, ...), custom_call_target="tpu_custom_call" | custom-call | flops 1073741824 | bytes 4718592 | tf_op jit(solution)/shard_map/pallas_call | solution.py:120
  36.5 0.9 %shard_map.53 = f32[8,128,128]{2,1,0:T(8,128)S(1)} custom-call(s32[8,128]{1,0:T(8,128)S(4)} %get-tuple-element.19.refs_0_, bf16[256,128,128]{2,1,0:T(8,128)(2,1)S(1)} %get-tuple-element.20.refs_1_, bf16[8,128,128]{2,1,0:T(8,128)(2,1)S(1)} %add_convert_fusion.2.refs_2_, bf16[8,128,128]{2,1,0:T(8,128)(2,1)S(1)} %collective-permute-done.11.refs_3_), custom_call_target="tpu_custom_call" | custom-call | flops 536870912 | bytes 2359296 | tf_op jit(solution)/shard_map/pallas_call | solution.py:120
  37.5 2.1 %collective-permute-start.14 = (bf16[8,128,128]{2,1,0:T(8,128)(2,1)S(1)}, bf16[8,128,128]{2,1,0:T(8,128)(2,1)S(1)}, u32[]{:S(2)}, u32[]{:S(2)}) collective-permute-start(bf16[8,128,128]{2,1,0:T(8,128)(2,1)S(1)} %add_convert_fusion.1), channel_id=1, source_target_pairs={{0,8},{4,12},{8,0},{12,4},{16,20},{20,16},{24,28},{28,24},{1,9},{5... | collective-permute-start | bytes 786440 | tf_op jit(solution)/shard_map/ppermute | solution.py:145
  39.6 2.3 %collective-permute-done.6 = bf16[8,128,128]{2,1,0:T(8,128)(2,1)S(1)} collective-permute-done((bf16[8,128,128]{2,1,0:T(8,128)(2,1)S(1)}, bf16[8,128,128]{2,1,0:T(8,128)(2,1)S(1)}, u32[]{:S(2)}, u32[]{:S(2)}) %collective-permute-start.6) | collective-permute-done | bytes 262176 | tf_op jit(solution)/shard_map/ppermute | solution.py:145
  41.9 1.4 %collective-permute-start.7 = (bf16[8,128,128]{2,1,0:T(8,128)(2,1)S(1)}, bf16[8,128,128]{2,1,0:T(8,128)(2,1)S(1)}, u32[]{:S(2)}, u32[]{:S(2)}) collective-permute-start(bf16[8,128,128]{2,1,0:T(8,128)(2,1)S(1)} %add_convert_fusion.5), channel_id=1, source_target_pairs={{0,8},{4,12},{8,0},{12,4},{16,20},{20,16},{24,28},{28,24},{1,9},{5... | collective-permute-start | bytes 786440 | tf_op jit(solution)/shard_map/ppermute | solution.py:145
  43.3 0.9 %shard_map.50 = f32[8,128,128]{2,1,0:T(8,128)S(1)} custom-call(s32[8,128]{1,0:T(8,128)S(4)} %get-tuple-element.19.refs_0_, bf16[256,128,128]{2,1,0:T(8,128)(2,1)S(1)} %get-tuple-element.20.refs_1_, bf16[8,128,128]{2,1,0:T(8,128)(2,1)S(1)} %add_convert_fusion.6.refs_2_, bf16[8,128,128]{2,1,0:T(8,128)(2,1)S(1)} %collective-permute-done.4.refs_3_), custom_call_target="tpu_custom_call" | custom-call | flops 536870912 | bytes 2359296 | tf_op jit(solution)/shard_map/pallas_call | solution.py:120
  44.2 1.6 %collective-permute-done.14 = bf16[8,128,128]{2,1,0:T(8,128)(2,1)S(1)} collective-permute-done((bf16[8,128,128]{2,1,0:T(8,128)(2,1)S(1)}, bf16[8,128,128]{2,1,0:T(8,128)(2,1)S(1)}, u32[]{:S(2)}, u32[]{:S(2)}) %collective-permute-start.14) | collective-permute-done | bytes 262176 | tf_op jit(solution)/shard_map/ppermute | solution.py:145
  45.8 1.6 %collective-permute-done.5 = bf16[8,128,128]{2,1,0:T(8,128)(2,1)S(1)} collective-permute-done((bf16[8,128,128]{2,1,0:T(8,128)(2,1)S(1)}, bf16[8,128,128]{2,1,0:T(8,128)(2,1)S(1)}, u32[]{:S(2)}, u32[]{:S(2)}) %collective-permute-start.5) | collective-permute-done | bytes 262176 | tf_op jit(solution)/shard_map/ppermute | solution.py:145
  47.4 1.1 %collective-permute-done.7 = bf16[8,128,128]{2,1,0:T(8,128)(2,1)S(1)} collective-permute-done((bf16[8,128,128]{2,1,0:T(8,128)(2,1)S(1)}, bf16[8,128,128]{2,1,0:T(8,128)(2,1)S(1)}, u32[]{:S(2)}, u32[]{:S(2)}) %collective-permute-start.7) | collective-permute-done | bytes 262176 | tf_op jit(solution)/shard_map/ppermute | solution.py:145
  (27 shorter events, 4.3 us)
Async XLA Ops:
  0.0 4.7 %copy-start = (bf16[1024,256]{1,0:T(8,128)(2,1)S(1)}, bf16[1024,256]{1,0:T(8,128)(2,1)}, u32[]{:S(2)}) copy-start(bf16[1024,256]{1,0:T(8,128)(2,1)} %param.4) | copy-start | bytes 1572868
  0.0 4.6 %collective-permute-start = (bf16[8,128,256]{2,1,0:T(8,128)(2,1)}, bf16[8,128,256]{2,1,0:T(8,128)(2,1)S(1)}, u32[]{:S(2)}, u32[]{:S(2)}) collective-permute-start(bf16[8,128,256]{2,1,0:T(8,128)(2,1)} %bitcast.6), channel_id=1, source_target_pairs={{0,16},{16,0},{1,17},{17,1},{2,18},{18,2},{3,19},{19,3},{4,20},{20... | collective-permute-start | bytes 1572872 | tf_op jit(solution)/shard_map/ppermute | solution.py:150
  5.7 7.0 %collective-permute-start.9 = (bf16[8,128,128]{2,1,0:T(8,128)(2,1)S(1)}, bf16[8,128,128]{2,1,0:T(8,128)(2,1)S(1)}, u32[]{:S(2)}, u32[]{:S(2)}) collective-permute-start(bf16[8,128,128]{2,1,0:T(8,128)(2,1)S(1)} %get-tuple-element.30), channel_id=1, source_target_pairs={{0,4},{4,0},{8,12},{12,8},{16,24},{20,28},{24,16},{28,20},{1,5},{5... | collective-permute-start | bytes 786440 | tf_op jit(solution)/shard_map/ppermute | solution.py:145
  8.3 7.2 %collective-permute-start.2 = (bf16[8,128,128]{2,1,0:T(8,128)(2,1)S(1)}, bf16[8,128,128]{2,1,0:T(8,128)(2,1)S(1)}, u32[]{:S(2)}, u32[]{:S(2)}) collective-permute-start(bf16[8,128,128]{2,1,0:T(8,128)(2,1)S(1)} %get-tuple-element.24), channel_id=1, source_target_pairs={{0,4},{4,0},{8,12},{12,8},{16,24},{20,28},{24,16},{28,20},{1,5},{5... | collective-permute-start | bytes 786440 | tf_op jit(solution)/shard_map/ppermute | solution.py:145
  10.2 10.9 %collective-permute-start.8 = (bf16[8,128,128]{2,1,0:T(8,128)(2,1)S(1)}, bf16[8,128,128]{2,1,0:T(8,128)(2,1)S(1)}, u32[]{:S(2)}, u32[]{:S(2)}) collective-permute-start(bf16[8,128,128]{2,1,0:T(8,128)(2,1)S(1)} %get-tuple-element.28), channel_id=1, source_target_pairs={{0,4},{4,0},{8,12},{12,8},{16,24},{20,28},{24,16},{28,20},{1,5},{5... | collective-permute-start | bytes 786440 | tf_op jit(solution)/shard_map/ppermute | solution.py:145
  12.2 14.4 %collective-permute-start.1 = (bf16[8,128,128]{2,1,0:T(8,128)(2,1)S(1)}, bf16[8,128,128]{2,1,0:T(8,128)(2,1)S(1)}, u32[]{:S(2)}, u32[]{:S(2)}) collective-permute-start(bf16[8,128,128]{2,1,0:T(8,128)(2,1)S(1)} %get-tuple-element.22), channel_id=1, source_target_pairs={{0,4},{4,0},{8,12},{12,8},{16,24},{20,28},{24,16},{28,20},{1,5},{5... | collective-permute-start | bytes 786440 | tf_op jit(solution)/shard_map/ppermute | solution.py:145
  12.7 9.3 %collective-permute-start.10 = (bf16[8,128,128]{2,1,0:T(8,128)(2,1)S(1)}, bf16[8,128,128]{2,1,0:T(8,128)(2,1)S(1)}, u32[]{:S(2)}, u32[]{:S(2)}) collective-permute-start(bf16[8,128,128]{2,1,0:T(8,128)(2,1)S(1)} %add_convert_fusion.3), channel_id=1, source_target_pairs={{0,8},{4,12},{8,0},{12,4},{16,20},{20,16},{24,28},{28,24},{1,9},{5... | collective-permute-start | bytes 786440 | tf_op jit(solution)/shard_map/ppermute | solution.py:145
  15.6 11.1 %collective-permute-start.3 = (bf16[8,128,128]{2,1,0:T(8,128)(2,1)S(1)}, bf16[8,128,128]{2,1,0:T(8,128)(2,1)S(1)}, u32[]{:S(2)}, u32[]{:S(2)}) collective-permute-start(bf16[8,128,128]{2,1,0:T(8,128)(2,1)S(1)} %add_convert_fusion.7), channel_id=1, source_target_pairs={{0,8},{4,12},{8,0},{12,4},{16,20},{20,16},{24,28},{28,24},{1,9},{5... | collective-permute-start | bytes 786440 | tf_op jit(solution)/shard_map/ppermute | solution.py:145
  22.1 4.7 %collective-permute-start.11 = (bf16[8,128,128]{2,1,0:T(8,128)(2,1)S(1)}, bf16[8,128,128]{2,1,0:T(8,128)(2,1)S(1)}, u32[]{:S(2)}, u32[]{:S(2)}) collective-permute-start(bf16[8,128,128]{2,1,0:T(8,128)(2,1)S(1)} %add_convert_fusion.2.refs_2_), channel_id=1, source_target_pairs={{0,16},{16,0},{1,17},{17,1},{2,18},{18,2},{3,19},{19,3},{4,20},{20... | collective-permute-start | bytes 786440 | tf_op jit(solution)/shard_map/ppermute | solution.py:150
  26.8 4.9 %collective-permute-start.4 = (bf16[8,128,128]{2,1,0:T(8,128)(2,1)S(1)}, bf16[8,128,128]{2,1,0:T(8,128)(2,1)S(1)}, u32[]{:S(2)}, u32[]{:S(2)}) collective-permute-start(bf16[8,128,128]{2,1,0:T(8,128)(2,1)S(1)} %add_convert_fusion.6.refs_2_), channel_id=1, source_target_pairs={{0,16},{16,0},{1,17},{17,1},{2,18},{18,2},{3,19},{19,3},{4,20},{20... | collective-permute-start | bytes 786440 | tf_op jit(solution)/shard_map/ppermute | solution.py:150
  27.8 9.6 %collective-permute-start.13 = (bf16[8,128,128]{2,1,0:T(8,128)(2,1)S(1)}, bf16[8,128,128]{2,1,0:T(8,128)(2,1)S(1)}, u32[]{:S(2)}, u32[]{:S(2)}) collective-permute-start(bf16[8,128,128]{2,1,0:T(8,128)(2,1)S(1)} %shard_map.55), channel_id=1, source_target_pairs={{0,4},{4,0},{8,12},{12,8},{16,24},{20,28},{24,16},{28,20},{1,5},{5... | collective-permute-start | bytes 786440 | tf_op jit(solution)/shard_map/ppermute | solution.py:145
  31.6 12.6 %collective-permute-start.12 = (bf16[8,128,128]{2,1,0:T(8,128)(2,1)S(1)}, bf16[8,128,128]{2,1,0:T(8,128)(2,1)S(1)}, u32[]{:S(2)}, u32[]{:S(2)}) collective-permute-start(bf16[8,128,128]{2,1,0:T(8,128)(2,1)S(1)} %get-tuple-element.31), channel_id=1, source_target_pairs={{0,4},{4,0},{8,12},{12,8},{16,24},{20,28},{24,16},{28,20},{1,5},{5... | collective-permute-start | bytes 786440 | tf_op jit(solution)/shard_map/ppermute | solution.py:145
  32.6 9.2 %collective-permute-start.6 = (bf16[8,128,128]{2,1,0:T(8,128)(2,1)S(1)}, bf16[8,128,128]{2,1,0:T(8,128)(2,1)S(1)}, u32[]{:S(2)}, u32[]{:S(2)}) collective-permute-start(bf16[8,128,128]{2,1,0:T(8,128)(2,1)S(1)} %shard_map.52), channel_id=1, source_target_pairs={{0,4},{4,0},{8,12},{12,8},{16,24},{20,28},{24,16},{28,20},{1,5},{5... | collective-permute-start | bytes 786440 | tf_op jit(solution)/shard_map/ppermute | solution.py:145
  36.4 11.0 %collective-permute-start.5 = (bf16[8,128,128]{2,1,0:T(8,128)(2,1)S(1)}, bf16[8,128,128]{2,1,0:T(8,128)(2,1)S(1)}, u32[]{:S(2)}, u32[]{:S(2)}) collective-permute-start(bf16[8,128,128]{2,1,0:T(8,128)(2,1)S(1)} %get-tuple-element.25), channel_id=1, source_target_pairs={{0,4},{4,0},{8,12},{12,8},{16,24},{20,28},{24,16},{28,20},{1,5},{5... | collective-permute-start | bytes 786440 | tf_op jit(solution)/shard_map/ppermute | solution.py:145
  37.5 8.3 %collective-permute-start.14 = (bf16[8,128,128]{2,1,0:T(8,128)(2,1)S(1)}, bf16[8,128,128]{2,1,0:T(8,128)(2,1)S(1)}, u32[]{:S(2)}, u32[]{:S(2)}) collective-permute-start(bf16[8,128,128]{2,1,0:T(8,128)(2,1)S(1)} %add_convert_fusion.1), channel_id=1, source_target_pairs={{0,8},{4,12},{8,0},{12,4},{16,20},{20,16},{24,28},{28,24},{1,9},{5... | collective-permute-start | bytes 786440 | tf_op jit(solution)/shard_map/ppermute | solution.py:145
  41.9 6.7 %collective-permute-start.7 = (bf16[8,128,128]{2,1,0:T(8,128)(2,1)S(1)}, bf16[8,128,128]{2,1,0:T(8,128)(2,1)S(1)}, u32[]{:S(2)}, u32[]{:S(2)}) collective-permute-start(bf16[8,128,128]{2,1,0:T(8,128)(2,1)S(1)} %add_convert_fusion.5), channel_id=1, source_target_pairs={{0,8},{4,12},{8,0},{12,4},{16,20},{20,16},{24,28},{28,24},{1,9},{5... | collective-permute-start | bytes 786440 | tf_op jit(solution)/shard_map/ppermute | solution.py:145

commit v3 on v2

--- a/solution.py
+++ b/solution.py
@@ -108,7 +108,7 @@
                 out[b] = total[:, j * CHUNK : (j + 1) * CHUNK].astype(out.dtype)
             return carry
 
-        lax.fori_loop(0, count, row, 0, unroll=4)
+        lax.fori_loop(0, count, row, 0, unroll=8)
         first += count
 
 
@@ -116,7 +116,6 @@
     blocks = sum(s.shape[0] for s in sources)
     columns = sources[0].shape[2]
     split = columns // CHUNK
-    rows, depth = sum(n for n, _ in outs), table.shape[0] * TILE_SIZE
     out = pl.pallas_call(
         functools.partial(sweep_kernel, [n for n, _ in outs], first, len(sources)),
         out_shape=[
@@ -126,11 +125,6 @@
         out_specs=[VMEM] * (len(outs) * split),
         scratch_shapes=[pltpu.VMEM((blocks + 1, TILE_SIZE, columns), jnp.bfloat16)],
         compiler_params=pltpu.CompilerParams(vmem_limit_bytes=12 << 20),
-        cost_estimate=pl.CostEstimate(
-            flops=2 * rows * TILE_SIZE * depth * columns * 2,
-            transcendentals=0,
-            bytes_accessed=rows * TILE_SIZE * (depth + columns) * 2,
-        ),
     )(table, tiles, *sources)
     return [out[i * split : (i + 1) * split] for i in range(len(outs))]
 

time: 49.8 us -> 49.1 us (0.986)
  Pallas kernels: 14.4 us -> 12.1 us
  starting transfers between devices: 17.7 us -> 19.1 us
  waiting for transfers between devices: 15 us -> 15.5 us
    pallas_call x9, Pallas kernels: 10.9 us -> 8.54 us  [sweep(): pl.pallas_call(functools.partial(sweep_kernel, [n for n, _ in outs], firs...]
    ppermute x12, starting transfers between devices: 17.1 us -> 18.5 us  [exchange(): return lax.ppermute(values, ('row', 'col'), pairs)]
  transfers between devices with their start and end apart: 15 -> 15, of which waited for: 9 -> 8; matrix products, arithmetic and copies ran while one was open for 1% -> 1% of each run, Pallas kernels for 27% -> 23%
where the time goes in v3:
time: 49.1 us; the launch traced here: 48.9 us
  starting transfers between devices  19.1 us (39%)
  waiting for transfers between devices  15.5 us (32%)
  Pallas kernels  12.1 us (25%)
  other arithmetic  1.46 us (3%)
  between operations  0.8 us (2%)
    ppermute x12, starting transfers between devices, exchange(): return lax.ppermute(values, ('row', 'col'), pairs)  18.5 us
    ppermute x12, waiting for transfers between devices, exchange(): return lax.ppermute(values, ('row', 'col'), pairs)  15.5 us
    pallas_call x9, Pallas kernels, sweep(): pl.pallas_call(functools.partial(sweep_kernel, [n for n, _ in outs], firs...  8.54 us
    pallas_call x1, Pallas kernels, load(): pl.pallas_call(functools.partial(load_kernel, own_first, share, blocks),...  3.53 us
  transfers between devices with their start and end apart: 15, of which 8 were waited for; matrix products, arithmetic and copies ran while one was open for 1% of the time, Pallas kernels for 23%

profile of v3, /device:TPU:0, one launch (start us, length us, event | category | flops | bytes accessed | tf_op | source)
XLA Modules:
  0.0 48.9 jit_solution(15339585929108352255)
XLA Ops:
  1.1 3.5 %shard_map.46 = (s32[8,128]{1,0:T(8,128)S(4)}, bf16[256,128,128]{2,1,0:T(8,128)(2,1)S(1)}) custom-call(s32[2,256]{1,0:T(2,128)} %bitcast.11, s32[1,1]{1,0:T(1,128)S(6)} %copy.5.count, bf16[256,128,128]{2,1,0:T(8,128)(2,1)} %bitcast.10), custom_call_target="tpu_custom_call" | custom-call | tf_op jit(solution)/shard_map/pallas_call | solution.py:68
  4.7 0.8 %shard_map.49 = (bf16[8,128,128]{2,1,0:T(8,128)(2,1)S(1)}, bf16[8,128,128]{2,1,0:T(8,128)(2,1)S(1)}) custom-call(s32[8,128]{1,0:T(8,128)S(4)} %get-tuple-element.19.refs_0_, bf16[256,128,128]{2,1,0:T(8,128)(2,1)S(1)} %get-tuple-element.20.refs_1_, bf16[8,128,256]{2,1,0:T(8,128)(2,1)S(1)} %bitcast.7, bf16[8,128,256]{2,1,0:T(8,128)(2,1)S(1)} %collective-permute-done.refs_3_), custom_call_target="tpu_custom_call" | custom-call | tf_op jit(solution)/shard_map/pallas_call | solution.py:119
  5.5 2.6 %collective-permute-start.9 = (bf16[8,128,128]{2,1,0:T(8,128)(2,1)S(1)}, bf16[8,128,128]{2,1,0:T(8,128)(2,1)S(1)}, u32[]{:S(2)}, u32[]{:S(2)}) collective-permute-start(bf16[8,128,128]{2,1,0:T(8,128)(2,1)S(1)} %get-tuple-element.30), channel_id=1, source_target_pairs={{0,4},{4,0},{8,12},{12,8},{16,24},{20,28},{24,16},{28,20},{1,5},{5... | collective-permute-start | bytes 786440 | tf_op jit(solution)/shard_map/ppermute | solution.py:139
  8.2 1.4 %shard_map.48 = (bf16[8,128,128]{2,1,0:T(8,128)(2,1)S(1)}, bf16[8,128,128]{2,1,0:T(8,128)(2,1)S(1)}, f32[8,128,128]{2,1,0:T(8,128)S(1)}, f32[8,128,128]{2,1,0:T(8,128)S(1)}) custom-call(s32[8,128]{1,0:T(8,128)S(4)} %get-tuple-element.19.refs_0_, bf16[256,128,128]{2,1,0:T(8,128)(2,1)S(1)} %get-tuple-element.20.refs_1_, bf16[8,128,256]{2,1,0:T(8,128)(2,1)S(1)} %bitcast.8, ...), custom_call_target="tpu_custom_call" | custom-call | tf_op jit(solution)/shard_map/pallas_call | solution.py:119
  9.6 2.0 %collective-permute-start.8 = (bf16[8,128,128]{2,1,0:T(8,128)(2,1)S(1)}, bf16[8,128,128]{2,1,0:T(8,128)(2,1)S(1)}, u32[]{:S(2)}, u32[]{:S(2)}) collective-permute-start(bf16[8,128,128]{2,1,0:T(8,128)(2,1)S(1)} %get-tuple-element.28), channel_id=1, source_target_pairs={{0,4},{4,0},{8,12},{12,8},{16,24},{20,28},{24,16},{28,20},{1,5},{5... | collective-permute-start | bytes 786440 | tf_op jit(solution)/shard_map/ppermute | solution.py:139
  11.6 0.8 %collective-permute-done.9 = bf16[8,128,128]{2,1,0:T(8,128)(2,1)S(1)} collective-permute-done((bf16[8,128,128]{2,1,0:T(8,128)(2,1)S(1)}, bf16[8,128,128]{2,1,0:T(8,128)(2,1)S(1)}, u32[]{:S(2)}, u32[]{:S(2)}) %collective-permute-start.9) | collective-permute-done | bytes 262176 | tf_op jit(solution)/shard_map/ppermute | solution.py:139
  12.5 2.1 %collective-permute-start.10 = (bf16[8,128,128]{2,1,0:T(8,128)(2,1)S(1)}, bf16[8,128,128]{2,1,0:T(8,128)(2,1)S(1)}, u32[]{:S(2)}, u32[]{:S(2)}) collective-permute-start(bf16[8,128,128]{2,1,0:T(8,128)(2,1)S(1)} %add_convert_fusion.3), channel_id=1, source_target_pairs={{0,8},{4,12},{8,0},{12,4},{16,20},{20,16},{24,28},{28,24},{1,9},{5... | collective-permute-start | bytes 786440 | tf_op jit(solution)/shard_map/ppermute | solution.py:139
  14.6 1.5 %collective-permute-start.1 = (bf16[8,128,128]{2,1,0:T(8,128)(2,1)S(1)}, bf16[8,128,128]{2,1,0:T(8,128)(2,1)S(1)}, u32[]{:S(2)}, u32[]{:S(2)}) collective-permute-start(bf16[8,128,128]{2,1,0:T(8,128)(2,1)S(1)} %get-tuple-element.22), channel_id=1, source_target_pairs={{0,4},{4,0},{8,12},{12,8},{16,24},{20,28},{24,16},{28,20},{1,5},{5... | collective-permute-start | bytes 786440 | tf_op jit(solution)/shard_map/ppermute | solution.py:139
  16.2 1.7 %collective-permute-start.3 = (bf16[8,128,128]{2,1,0:T(8,128)(2,1)S(1)}, bf16[8,128,128]{2,1,0:T(8,128)(2,1)S(1)}, u32[]{:S(2)}, u32[]{:S(2)}) collective-permute-start(bf16[8,128,128]{2,1,0:T(8,128)(2,1)S(1)} %add_convert_fusion.7), channel_id=1, source_target_pairs={{0,8},{4,12},{8,0},{12,4},{16,20},{20,16},{24,28},{28,24},{1,9},{5... | collective-permute-start | bytes 786440 | tf_op jit(solution)/shard_map/ppermute | solution.py:139
  17.9 0.8 %shard_map.47 = (f32[8,128,128]{2,1,0:T(8,128)S(1)}, f32[8,128,128]{2,1,0:T(8,128)S(1)}) custom-call(s32[8,128]{1,0:T(8,128)S(4)} %get-tuple-element.19.refs_0_, bf16[256,128,128]{2,1,0:T(8,128)(2,1)S(1)} %get-tuple-element.20.refs_1_, bf16[8,128,256]{2,1,0:T(8,128)(2,1)S(1)} %bitcast.9, bf16[8,128,256]{2,1,0:T(8,128)(2,1)S(1)} %collective-permute-done.refs_3_), custom_call_target="tpu_custom_call" | custom-call | tf_op jit(solution)/shard_map/pallas_call | solution.py:119
  18.7 2.3 %collective-permute-done.8 = bf16[8,128,128]{2,1,0:T(8,128)(2,1)S(1)} collective-permute-done((bf16[8,128,128]{2,1,0:T(8,128)(2,1)S(1)}, bf16[8,128,128]{2,1,0:T(8,128)(2,1)S(1)}, u32[]{:S(2)}, u32[]{:S(2)}) %collective-permute-start.8) | collective-permute-done | bytes 262176 | tf_op jit(solution)/shard_map/ppermute | solution.py:139
  21.0 0.9 %collective-permute-done.10 = bf16[8,128,128]{2,1,0:T(8,128)(2,1)S(1)} collective-permute-done((bf16[8,128,128]{2,1,0:T(8,128)(2,1)S(1)}, bf16[8,128,128]{2,1,0:T(8,128)(2,1)S(1)}, u32[]{:S(2)}, u32[]{:S(2)}) %collective-permute-start.10) | collective-permute-done | bytes 262176 | tf_op jit(solution)/shard_map/ppermute | solution.py:139
  22.0 4.5 %collective-permute-done.1 = bf16[8,128,128]{2,1,0:T(8,128)(2,1)S(1)} collective-permute-done((bf16[8,128,128]{2,1,0:T(8,128)(2,1)S(1)}, bf16[8,128,128]{2,1,0:T(8,128)(2,1)S(1)}, u32[]{:S(2)}, u32[]{:S(2)}) %collective-permute-start.1) | collective-permute-done | bytes 262176 | tf_op jit(solution)/shard_map/ppermute | solution.py:139
  27.4 2.1 %collective-permute-start.13 = (bf16[8,128,128]{2,1,0:T(8,128)(2,1)S(1)}, bf16[8,128,128]{2,1,0:T(8,128)(2,1)S(1)}, u32[]{:S(2)}, u32[]{:S(2)}) collective-permute-start(bf16[8,128,128]{2,1,0:T(8,128)(2,1)S(1)} %shard_map.55), channel_id=1, source_target_pairs={{0,4},{4,0},{8,12},{12,8},{16,24},{20,28},{24,16},{28,20},{1,5},{5... | collective-permute-start | bytes 786440 | tf_op jit(solution)/shard_map/ppermute | solution.py:139
  30.3 0.8 %collective-permute-start.6 = (bf16[8,128,128]{2,1,0:T(8,128)(2,1)S(1)}, bf16[8,128,128]{2,1,0:T(8,128)(2,1)S(1)}, u32[]{:S(2)}, u32[]{:S(2)}) collective-permute-start(bf16[8,128,128]{2,1,0:T(8,128)(2,1)S(1)} %shard_map.52), channel_id=1, source_target_pairs={{0,4},{4,0},{8,12},{12,8},{16,24},{20,28},{24,16},{28,20},{1,5},{5... | collective-permute-start | bytes 786440 | tf_op jit(solution)/shard_map/ppermute | solution.py:139
  31.0 1.3 %shard_map.54 = (bf16[8,128,128]{2,1,0:T(8,128)(2,1)S(1)}, f32[8,128,128]{2,1,0:T(8,128)S(1)}) custom-call(s32[8,128]{1,0:T(8,128)S(4)} %get-tuple-element.19.refs_0_, bf16[256,128,128]{2,1,0:T(8,128)(2,1)S(1)} %get-tuple-element.20.refs_1_, bf16[8,128,128]{2,1,0:T(8,128)(2,1)S(1)} %add_convert_fusion.2.refs_2_, ...), custom_call_target="tpu_custom_call" | custom-call | tf_op jit(solution)/shard_map/pallas_call | solution.py:119
  32.3 1.4 %collective-permute-start.12 = (bf16[8,128,128]{2,1,0:T(8,128)(2,1)S(1)}, bf16[8,128,128]{2,1,0:T(8,128)(2,1)S(1)}, u32[]{:S(2)}, u32[]{:S(2)}) collective-permute-start(bf16[8,128,128]{2,1,0:T(8,128)(2,1)S(1)} %get-tuple-element.31), channel_id=1, source_target_pairs={{0,4},{4,0},{8,12},{12,8},{16,24},{20,28},{24,16},{28,20},{1,5},{5... | collective-permute-start | bytes 786440 | tf_op jit(solution)/shard_map/ppermute | solution.py:139
  33.9 2.1 %collective-permute-start.14 = (bf16[8,128,128]{2,1,0:T(8,128)(2,1)S(1)}, bf16[8,128,128]{2,1,0:T(8,128)(2,1)S(1)}, u32[]{:S(2)}, u32[]{:S(2)}) collective-permute-start(bf16[8,128,128]{2,1,0:T(8,128)(2,1)S(1)} %add_convert_fusion.1), channel_id=1, source_target_pairs={{0,8},{4,12},{8,0},{12,4},{16,20},{20,16},{24,28},{28,24},{1,9},{5... | collective-permute-start | bytes 786440 | tf_op jit(solution)/shard_map/ppermute | solution.py:139
  36.1 1.3 %shard_map.51 = (bf16[8,128,128]{2,1,0:T(8,128)(2,1)S(1)}, f32[8,128,128]{2,1,0:T(8,128)S(1)}) custom-call(s32[8,128]{1,0:T(8,128)S(4)} %get-tuple-element.19.refs_0_, bf16[256,128,128]{2,1,0:T(8,128)(2,1)S(1)} %get-tuple-element.20.refs_1_, bf16[8,128,128]{2,1,0:T(8,128)(2,1)S(1)} %add_convert_fusion.6.refs_2_, ...), custom_call_target="tpu_custom_call" | custom-call | tf_op jit(solution)/shard_map/pallas_call | solution.py:119
  37.3 1.6 %collective-permute-start.5 = (bf16[8,128,128]{2,1,0:T(8,128)(2,1)S(1)}, bf16[8,128,128]{2,1,0:T(8,128)(2,1)S(1)}, u32[]{:S(2)}, u32[]{:S(2)}) collective-permute-start(bf16[8,128,128]{2,1,0:T(8,128)(2,1)S(1)} %get-tuple-element.25), channel_id=1, source_target_pairs={{0,4},{4,0},{8,12},{12,8},{16,24},{20,28},{24,16},{28,20},{1,5},{5... | collective-permute-start | bytes 786440 | tf_op jit(solution)/shard_map/ppermute | solution.py:139
  41.0 1.4 %collective-permute-done.12 = bf16[8,128,128]{2,1,0:T(8,128)(2,1)S(1)} collective-permute-done((bf16[8,128,128]{2,1,0:T(8,128)(2,1)S(1)}, bf16[8,128,128]{2,1,0:T(8,128)(2,1)S(1)}, u32[]{:S(2)}, u32[]{:S(2)}) %collective-permute-start.12) | collective-permute-done | bytes 262176 | tf_op jit(solution)/shard_map/ppermute | solution.py:139
  42.4 0.9 %collective-permute-done.14 = bf16[8,128,128]{2,1,0:T(8,128)(2,1)S(1)} collective-permute-done((bf16[8,128,128]{2,1,0:T(8,128)(2,1)S(1)}, bf16[8,128,128]{2,1,0:T(8,128)(2,1)S(1)}, u32[]{:S(2)}, u32[]{:S(2)}) %collective-permute-start.14) | collective-permute-done | bytes 262176 | tf_op jit(solution)/shard_map/ppermute | solution.py:139
  43.4 4.6 %collective-permute-done.5 = bf16[8,128,128]{2,1,0:T(8,128)(2,1)S(1)} collective-permute-done((bf16[8,128,128]{2,1,0:T(8,128)(2,1)S(1)}, bf16[8,128,128]{2,1,0:T(8,128)(2,1)S(1)}, u32[]{:S(2)}, u32[]{:S(2)}) %collective-permute-start.5) | collective-permute-done | bytes 262176 | tf_op jit(solution)/shard_map/ppermute | solution.py:139
  48.0 0.9 %pad_maximum_fusion = bf16[8,128,256]{2,1,0:T(8,128)(2,1)} fusion(bf16[8,128,128]{2,1,0:T(8,128)(2,1)S(1)} %add_convert_fusion, bf16[8,128,128]{2,1,0:T(8,128)(2,1)S(1)} %add_convert_fusion.4), kind=kLoop, calls=%fused_computation | loop fusion | flops 1048576 | bytes 1048576 | tf_op jit(solution)/shard_map/concatenate | solution.py:173
  (27 shorter events, 5.0 us)
Async XLA Ops:
  0.0 4.7 %copy-start = (bf16[1024,256]{1,0:T(8,128)(2,1)S(1)}, bf16[1024,256]{1,0:T(8,128)(2,1)}, u32[]{:S(2)}) copy-start(bf16[1024,256]{1,0:T(8,128)(2,1)} %param.4) | copy-start | bytes 1572868
  0.0 4.6 %collective-permute-start = (bf16[8,128,256]{2,1,0:T(8,128)(2,1)}, bf16[8,128,256]{2,1,0:T(8,128)(2,1)S(1)}, u32[]{:S(2)}, u32[]{:S(2)}) collective-permute-start(bf16[8,128,256]{2,1,0:T(8,128)(2,1)} %bitcast.6), channel_id=1, source_target_pairs={{0,16},{16,0},{1,17},{17,1},{2,18},{18,2},{3,19},{19,3},{4,20},{20... | collective-permute-start | bytes 1572872 | tf_op jit(solution)/shard_map/ppermute | solution.py:144
  5.5 7.0 %collective-permute-start.9 = (bf16[8,128,128]{2,1,0:T(8,128)(2,1)S(1)}, bf16[8,128,128]{2,1,0:T(8,128)(2,1)S(1)}, u32[]{:S(2)}, u32[]{:S(2)}) collective-permute-start(bf16[8,128,128]{2,1,0:T(8,128)(2,1)S(1)} %get-tuple-element.30), channel_id=1, source_target_pairs={{0,4},{4,0},{8,12},{12,8},{16,24},{20,28},{24,16},{28,20},{1,5},{5... | collective-permute-start | bytes 786440 | tf_op jit(solution)/shard_map/ppermute | solution.py:139
  8.1 8.0 %collective-permute-start.2 = (bf16[8,128,128]{2,1,0:T(8,128)(2,1)S(1)}, bf16[8,128,128]{2,1,0:T(8,128)(2,1)S(1)}, u32[]{:S(2)}, u32[]{:S(2)}) collective-permute-start(bf16[8,128,128]{2,1,0:T(8,128)(2,1)S(1)} %get-tuple-element.24), channel_id=1, source_target_pairs={{0,4},{4,0},{8,12},{12,8},{16,24},{20,28},{24,16},{28,20},{1,5},{5... | collective-permute-start | bytes 786440 | tf_op jit(solution)/shard_map/ppermute | solution.py:139
  9.6 11.4 %collective-permute-start.8 = (bf16[8,128,128]{2,1,0:T(8,128)(2,1)S(1)}, bf16[8,128,128]{2,1,0:T(8,128)(2,1)S(1)}, u32[]{:S(2)}, u32[]{:S(2)}) collective-permute-start(bf16[8,128,128]{2,1,0:T(8,128)(2,1)S(1)} %get-tuple-element.28), channel_id=1, source_target_pairs={{0,4},{4,0},{8,12},{12,8},{16,24},{20,28},{24,16},{28,20},{1,5},{5... | collective-permute-start | bytes 786440 | tf_op jit(solution)/shard_map/ppermute | solution.py:139
  12.5 9.3 %collective-permute-start.10 = (bf16[8,128,128]{2,1,0:T(8,128)(2,1)S(1)}, bf16[8,128,128]{2,1,0:T(8,128)(2,1)S(1)}, u32[]{:S(2)}, u32[]{:S(2)}) collective-permute-start(bf16[8,128,128]{2,1,0:T(8,128)(2,1)S(1)} %add_convert_fusion.3), channel_id=1, source_target_pairs={{0,8},{4,12},{8,0},{12,4},{16,20},{20,16},{24,28},{28,24},{1,9},{5... | collective-permute-start | bytes 786440 | tf_op jit(solution)/shard_map/ppermute | solution.py:139
  14.6 11.9 %collective-permute-start.1 = (bf16[8,128,128]{2,1,0:T(8,128)(2,1)S(1)}, bf16[8,128,128]{2,1,0:T(8,128)(2,1)S(1)}, u32[]{:S(2)}, u32[]{:S(2)}) collective-permute-start(bf16[8,128,128]{2,1,0:T(8,128)(2,1)S(1)} %get-tuple-element.22), channel_id=1, source_target_pairs={{0,4},{4,0},{8,12},{12,8},{16,24},{20,28},{24,16},{28,20},{1,5},{5... | collective-permute-start | bytes 786440 | tf_op jit(solution)/shard_map/ppermute | solution.py:139
  16.2 10.3 %collective-permute-start.3 = (bf16[8,128,128]{2,1,0:T(8,128)(2,1)S(1)}, bf16[8,128,128]{2,1,0:T(8,128)(2,1)S(1)}, u32[]{:S(2)}, u32[]{:S(2)}) collective-permute-start(bf16[8,128,128]{2,1,0:T(8,128)(2,1)S(1)} %add_convert_fusion.7), channel_id=1, source_target_pairs={{0,8},{4,12},{8,0},{12,4},{16,20},{20,16},{24,28},{28,24},{1,9},{5... | collective-permute-start | bytes 786440 | tf_op jit(solution)/shard_map/ppermute | solution.py:139
  22.0 4.7 %collective-permute-start.11 = (bf16[8,128,128]{2,1,0:T(8,128)(2,1)S(1)}, bf16[8,128,128]{2,1,0:T(8,128)(2,1)S(1)}, u32[]{:S(2)}, u32[]{:S(2)}) collective-permute-start(bf16[8,128,128]{2,1,0:T(8,128)(2,1)S(1)} %add_convert_fusion.2.refs_2_), channel_id=1, source_target_pairs={{0,16},{16,0},{1,17},{17,1},{2,18},{18,2},{3,19},{19,3},{4,20},{20... | collective-permute-start | bytes 786440 | tf_op jit(solution)/shard_map/ppermute | solution.py:144
  26.6 2.9 %collective-permute-start.4 = (bf16[8,128,128]{2,1,0:T(8,128)(2,1)S(1)}, bf16[8,128,128]{2,1,0:T(8,128)(2,1)S(1)}, u32[]{:S(2)}, u32[]{:S(2)}) collective-permute-start(bf16[8,128,128]{2,1,0:T(8,128)(2,1)S(1)} %add_convert_fusion.6.refs_2_), channel_id=1, source_target_pairs={{0,16},{16,0},{1,17},{17,1},{2,18},{18,2},{3,19},{19,3},{4,20},{20... | collective-permute-start | bytes 786440 | tf_op jit(solution)/shard_map/ppermute | solution.py:144
  27.4 6.4 %collective-permute-start.13 = (bf16[8,128,128]{2,1,0:T(8,128)(2,1)S(1)}, bf16[8,128,128]{2,1,0:T(8,128)(2,1)S(1)}, u32[]{:S(2)}, u32[]{:S(2)}) collective-permute-start(bf16[8,128,128]{2,1,0:T(8,128)(2,1)S(1)} %shard_map.55), channel_id=1, source_target_pairs={{0,4},{4,0},{8,12},{12,8},{16,24},{20,28},{24,16},{28,20},{1,5},{5... | collective-permute-start | bytes 786440 | tf_op jit(solution)/shard_map/ppermute | solution.py:139
  30.3 8.6 %collective-permute-start.6 = (bf16[8,128,128]{2,1,0:T(8,128)(2,1)S(1)}, bf16[8,128,128]{2,1,0:T(8,128)(2,1)S(1)}, u32[]{:S(2)}, u32[]{:S(2)}) collective-permute-start(bf16[8,128,128]{2,1,0:T(8,128)(2,1)S(1)} %shard_map.52), channel_id=1, source_target_pairs={{0,4},{4,0},{8,12},{12,8},{16,24},{20,28},{24,16},{28,20},{1,5},{5... | collective-permute-start | bytes 786440 | tf_op jit(solution)/shard_map/ppermute | solution.py:139
  32.3 10.1 %collective-permute-start.12 = (bf16[8,128,128]{2,1,0:T(8,128)(2,1)S(1)}, bf16[8,128,128]{2,1,0:T(8,128)(2,1)S(1)}, u32[]{:S(2)}, u32[]{:S(2)}) collective-permute-start(bf16[8,128,128]{2,1,0:T(8,128)(2,1)S(1)} %get-tuple-element.31), channel_id=1, source_target_pairs={{0,4},{4,0},{8,12},{12,8},{16,24},{20,28},{24,16},{28,20},{1,5},{5... | collective-permute-start | bytes 786440 | tf_op jit(solution)/shard_map/ppermute | solution.py:139
  33.9 9.3 %collective-permute-start.14 = (bf16[8,128,128]{2,1,0:T(8,128)(2,1)S(1)}, bf16[8,128,128]{2,1,0:T(8,128)(2,1)S(1)}, u32[]{:S(2)}, u32[]{:S(2)}) collective-permute-start(bf16[8,128,128]{2,1,0:T(8,128)(2,1)S(1)} %add_convert_fusion.1), channel_id=1, source_target_pairs={{0,8},{4,12},{8,0},{12,4},{16,20},{20,16},{24,28},{28,24},{1,9},{5... | collective-permute-start | bytes 786440 | tf_op jit(solution)/shard_map/ppermute | solution.py:139
  37.3 10.6 %collective-permute-start.5 = (bf16[8,128,128]{2,1,0:T(8,128)(2,1)S(1)}, bf16[8,128,128]{2,1,0:T(8,128)(2,1)S(1)}, u32[]{:S(2)}, u32[]{:S(2)}) collective-permute-start(bf16[8,128,128]{2,1,0:T(8,128)(2,1)S(1)} %get-tuple-element.25), channel_id=1, source_target_pairs={{0,4},{4,0},{8,12},{12,8},{16,24},{20,28},{24,16},{28,20},{1,5},{5... | collective-permute-start | bytes 786440 | tf_op jit(solution)/shard_map/ppermute | solution.py:139
  39.0 9.0 %collective-permute-start.7 = (bf16[8,128,128]{2,1,0:T(8,128)(2,1)S(1)}, bf16[8,128,128]{2,1,0:T(8,128)(2,1)S(1)}, u32[]{:S(2)}, u32[]{:S(2)}) collective-permute-start(bf16[8,128,128]{2,1,0:T(8,128)(2,1)S(1)} %add_convert_fusion.5), channel_id=1, source_target_pairs={{0,8},{4,12},{8,0},{12,4},{16,20},{20,16},{24,28},{28,24},{1,9},{5... | collective-permute-start | bytes 786440 | tf_op jit(solution)/shard_map/ppermute | solution.py:139

commit v4 on v3

--- a/solution.py
+++ b/solution.py
@@ -129,6 +129,37 @@
     return [out[i * split : (i + 1) * split] for i in range(len(outs))]
 
 
+def finish_kernel(column, own, near, last, *refs):
+    out, here, sem = refs[-3:]
+    count = own.shape[0]
+    copies = []
+    for b in range(count):
+        total = own[b] + near[b].astype(jnp.float32) + last[b].astype(jnp.float32)
+        rows = slice(b * TILE_SIZE, (b + 1) * TILE_SIZE)
+        here[rows] = total.astype(here.dtype)
+        copies.append(
+            pltpu.make_async_copy(here.at[rows], out.at[rows, column : column + CHUNK], sem.at[b])
+        )
+        copies[-1].start()
+    for copy in copies:
+        copy.wait()
+
+
+def finish(own, near, last, column, shape, earlier):
+    return pl.pallas_call(
+        functools.partial(finish_kernel, column),
+        out_shape=pltpu.HBM(shape, jnp.bfloat16),
+        in_specs=[VMEM] * 3 + [HBM] * len(earlier),
+        out_specs=HBM,
+        input_output_aliases={3: 0} if earlier else {},
+        scratch_shapes=[
+            pltpu.VMEM((shape[0], CHUNK), jnp.bfloat16),
+            pltpu.SemaphoreType.DMA((own.shape[0],)),
+        ],
+        compiler_params=pltpu.CompilerParams(vmem_limit_bytes=8 << 20),
+    )(own, near, last, *earlier)
+
+
 def exchange(values, second, n_row, n_col):
     pairs = []
     for r in range(n_row):
@@ -166,11 +197,14 @@
         near = [first(n) for n in near]
         (own,) = sweep(table, tiles, source, 3 * share, [(share, f32)])
         last = [second((k + f.astype(f32)).astype(bf16)) for k, f in zip(kept, far)]
-        return [(o + n.astype(f32) + t.astype(f32)).astype(bf16) for o, n, t in zip(own, near, last)]
-
-    once = couple(whole)
-    twice = [couple(panel_of(o, n_row))[0] for o in once]
-    return jnp.concatenate(twice, -1).reshape(source_columns.shape)
+        return list(zip(own, near, last))
+
+    once = [(o + n.astype(f32) + t.astype(f32)).astype(bf16) for o, n, t in couple(whole)]
+    parts = [couple(panel_of(o, n_row))[0] for o in once]
+    twice = []
+    for i, part in enumerate(parts):
+        twice = [finish(*part, i * CHUNK, source_columns.shape, twice)]
+    return twice[0]
 
 
 def solution(mesh):

time: 49.1 us -> 48.7 us (level)
  Pallas kernels: 12.1 us -> 13.6 us
  other arithmetic: 1.46 us -> 0.41 us
  starting transfers between devices: 19.1 us -> 18.6 us
    pallas_call x0 -> x2, Pallas kernels: none -> 1.54 us  [finish(): pl.pallas_call(functools.partial(finish_kernel, column), out_shape=pltpu....]
    concatenate x1 -> x0, other arithmetic: 0.86 us -> none  [local(): return jnp.concatenate(twice, -1).reshape(source_columns.shape)]
    ppermute x12, starting transfers between devices: 18.5 us -> 18 us  [exchange(): return lax.ppermute(values, ('row', 'col'), pairs)]
  transfers between devices with their start and end apart: 15 -> 15, of which waited for: 8 -> 8; matrix products, arithmetic and copies ran while one was open for 1% -> 1% of each run, Pallas kernels for 23% -> 25%
where the time goes in v4:
time: 48.7 us; the launch traced here: 48.5 us
  starting transfers between devices  18.6 us (38%)
  waiting for transfers between devices  15.1 us (31%)
  Pallas kernels  13.6 us (28%)
  between operations  0.8 us (2%)
    ppermute x12, starting transfers between devices, exchange(): return lax.ppermute(values, ('row', 'col'), pairs)  18 us
    ppermute x12, waiting for transfers between devices, exchange(): return lax.ppermute(values, ('row', 'col'), pairs)  15.1 us
    pallas_call x9, Pallas kernels, sweep(): pl.pallas_call(functools.partial(sweep_kernel, [n for n, _ in outs], firs...  8.54 us
    pallas_call x1, Pallas kernels, load(): pl.pallas_call(functools.partial(load_kernel, own_first, share, blocks),...  3.53 us
    pallas_call x2, Pallas kernels, finish(): pl.pallas_call(functools.partial(finish_kernel, column), out_shape=pltpu....  1.54 us
  transfers between devices with their start and end apart: 15, of which 8 were waited for; matrix products, arithmetic and copies ran while one was open for 1% of the time, Pallas kernels for 25%

profile of v4, /device:TPU:0, one launch (start us, length us, event | category | flops | bytes accessed | tf_op | source)
XLA Modules:
  0.0 48.5 jit_solution(4622402804258580985)
XLA Ops:
  1.1 3.5 %shard_map.46 = (s32[8,128]{1,0:T(8,128)S(4)}, bf16[256,128,128]{2,1,0:T(8,128)(2,1)S(1)}) custom-call(s32[2,256]{1,0:T(2,128)} %bitcast.10, s32[1,1]{1,0:T(1,128)S(6)} %copy.7.count, bf16[256,128,128]{2,1,0:T(8,128)(2,1)} %bitcast.9), custom_call_target="tpu_custom_call" | custom-call | tf_op jit(solution)/shard_map/pallas_call | solution.py:68
  4.7 0.8 %shard_map.49 = (bf16[8,128,128]{2,1,0:T(8,128)(2,1)S(1)}, bf16[8,128,128]{2,1,0:T(8,128)(2,1)S(1)}) custom-call(s32[8,128]{1,0:T(8,128)S(4)} %get-tuple-element.19.refs_0_, bf16[256,128,128]{2,1,0:T(8,128)(2,1)S(1)} %get-tuple-element.20.refs_1_, bf16[8,128,256]{2,1,0:T(8,128)(2,1)S(1)} %bitcast.6, bf16[8,128,256]{2,1,0:T(8,128)(2,1)S(1)} %collective-permute-done.refs_3_), custom_call_target="tpu_custom_call" | custom-call | tf_op jit(solution)/shard_map/pallas_call | solution.py:119
  5.5 2.6 %collective-permute-start.9 = (bf16[8,128,128]{2,1,0:T(8,128)(2,1)S(1)}, bf16[8,128,128]{2,1,0:T(8,128)(2,1)S(1)}, u32[]{:S(2)}, u32[]{:S(2)}) collective-permute-start(bf16[8,128,128]{2,1,0:T(8,128)(2,1)S(1)} %get-tuple-element.30), channel_id=1, source_target_pairs={{0,4},{4,0},{8,12},{12,8},{16,24},{20,28},{24,16},{28,20},{1,5},{5... | collective-permute-start | bytes 786440 | tf_op jit(solution)/shard_map/ppermute | solution.py:170
  8.2 1.4 %shard_map.48 = (bf16[8,128,128]{2,1,0:T(8,128)(2,1)S(1)}, bf16[8,128,128]{2,1,0:T(8,128)(2,1)S(1)}, f32[8,128,128]{2,1,0:T(8,128)S(1)}, f32[8,128,128]{2,1,0:T(8,128)S(1)}) custom-call(s32[8,128]{1,0:T(8,128)S(4)} %get-tuple-element.19.refs_0_, bf16[256,128,128]{2,1,0:T(8,128)(2,1)S(1)} %get-tuple-element.20.refs_1_, bf16[8,128,256]{2,1,0:T(8,128)(2,1)S(1)} %bitcast.7, ...), custom_call_target="tpu_custom_call" | custom-call | tf_op jit(solution)/shard_map/pallas_call | solution.py:119
  9.6 2.0 %collective-permute-start.8 = (bf16[8,128,128]{2,1,0:T(8,128)(2,1)S(1)}, bf16[8,128,128]{2,1,0:T(8,128)(2,1)S(1)}, u32[]{:S(2)}, u32[]{:S(2)}) collective-permute-start(bf16[8,128,128]{2,1,0:T(8,128)(2,1)S(1)} %get-tuple-element.28), channel_id=1, source_target_pairs={{0,4},{4,0},{8,12},{12,8},{16,24},{20,28},{24,16},{28,20},{1,5},{5... | collective-permute-start | bytes 786440 | tf_op jit(solution)/shard_map/ppermute | solution.py:170
  11.6 0.8 %collective-permute-done.9 = bf16[8,128,128]{2,1,0:T(8,128)(2,1)S(1)} collective-permute-done((bf16[8,128,128]{2,1,0:T(8,128)(2,1)S(1)}, bf16[8,128,128]{2,1,0:T(8,128)(2,1)S(1)}, u32[]{:S(2)}, u32[]{:S(2)}) %collective-permute-start.9) | collective-permute-done | bytes 262176 | tf_op jit(solution)/shard_map/ppermute | solution.py:170
  12.5 2.1 %collective-permute-start.10 = (bf16[8,128,128]{2,1,0:T(8,128)(2,1)S(1)}, bf16[8,128,128]{2,1,0:T(8,128)(2,1)S(1)}, u32[]{:S(2)}, u32[]{:S(2)}) collective-permute-start(bf16[8,128,128]{2,1,0:T(8,128)(2,1)S(1)} %add_convert_fusion.2), channel_id=1, source_target_pairs={{0,8},{4,12},{8,0},{12,4},{16,20},{20,16},{24,28},{28,24},{1,9},{5... | collective-permute-start | bytes 786440 | tf_op jit(solution)/shard_map/ppermute | solution.py:170
  14.6 1.5 %collective-permute-start.1 = (bf16[8,128,128]{2,1,0:T(8,128)(2,1)S(1)}, bf16[8,128,128]{2,1,0:T(8,128)(2,1)S(1)}, u32[]{:S(2)}, u32[]{:S(2)}) collective-permute-start(bf16[8,128,128]{2,1,0:T(8,128)(2,1)S(1)} %get-tuple-element.22), channel_id=1, source_target_pairs={{0,4},{4,0},{8,12},{12,8},{16,24},{20,28},{24,16},{28,20},{1,5},{5... | collective-permute-start | bytes 786440 | tf_op jit(solution)/shard_map/ppermute | solution.py:170
  16.2 1.7 %collective-permute-start.3 = (bf16[8,128,128]{2,1,0:T(8,128)(2,1)S(1)}, bf16[8,128,128]{2,1,0:T(8,128)(2,1)S(1)}, u32[]{:S(2)}, u32[]{:S(2)}) collective-permute-start(bf16[8,128,128]{2,1,0:T(8,128)(2,1)S(1)} %add_convert_fusion.5), channel_id=1, source_target_pairs={{0,8},{4,12},{8,0},{12,4},{16,20},{20,16},{24,28},{28,24},{1,9},{5... | collective-permute-start | bytes 786440 | tf_op jit(solution)/shard_map/ppermute | solution.py:170
  17.9 0.8 %shard_map.47 = (f32[8,128,128]{2,1,0:T(8,128)S(1)}, f32[8,128,128]{2,1,0:T(8,128)S(1)}) custom-call(s32[8,128]{1,0:T(8,128)S(4)} %get-tuple-element.19.refs_0_, bf16[256,128,128]{2,1,0:T(8,128)(2,1)S(1)} %get-tuple-element.20.refs_1_, bf16[8,128,256]{2,1,0:T(8,128)(2,1)S(1)} %bitcast.8, bf16[8,128,256]{2,1,0:T(8,128)(2,1)S(1)} %collective-permute-done.refs_3_), custom_call_target="tpu_custom_call" | custom-call | tf_op jit(solution)/shard_map/pallas_call | solution.py:119
  18.7 2.3 %collective-permute-done.8 = bf16[8,128,128]{2,1,0:T(8,128)(2,1)S(1)} collective-permute-done((bf16[8,128,128]{2,1,0:T(8,128)(2,1)S(1)}, bf16[8,128,128]{2,1,0:T(8,128)(2,1)S(1)}, u32[]{:S(2)}, u32[]{:S(2)}) %collective-permute-start.8) | collective-permute-done | bytes 262176 | tf_op jit(solution)/shard_map/ppermute | solution.py:170
  21.0 0.9 %collective-permute-done.10 = bf16[8,128,128]{2,1,0:T(8,128)(2,1)S(1)} collective-permute-done((bf16[8,128,128]{2,1,0:T(8,128)(2,1)S(1)}, bf16[8,128,128]{2,1,0:T(8,128)(2,1)S(1)}, u32[]{:S(2)}, u32[]{:S(2)}) %collective-permute-start.10) | collective-permute-done | bytes 262176 | tf_op jit(solution)/shard_map/ppermute | solution.py:170
  22.0 4.5 %collective-permute-done.1 = bf16[8,128,128]{2,1,0:T(8,128)(2,1)S(1)} collective-permute-done((bf16[8,128,128]{2,1,0:T(8,128)(2,1)S(1)}, bf16[8,128,128]{2,1,0:T(8,128)(2,1)S(1)}, u32[]{:S(2)}, u32[]{:S(2)}) %collective-permute-start.1) | collective-permute-done | bytes 262176 | tf_op jit(solution)/shard_map/ppermute | solution.py:170
  27.4 2.1 %collective-permute-start.13 = (bf16[8,128,128]{2,1,0:T(8,128)(2,1)S(1)}, bf16[8,128,128]{2,1,0:T(8,128)(2,1)S(1)}, u32[]{:S(2)}, u32[]{:S(2)}) collective-permute-start(bf16[8,128,128]{2,1,0:T(8,128)(2,1)S(1)} %shard_map.55), channel_id=1, source_target_pairs={{0,4},{4,0},{8,12},{12,8},{16,24},{20,28},{24,16},{28,20},{1,5},{5... | collective-permute-start | bytes 786440 | tf_op jit(solution)/shard_map/ppermute | solution.py:170
  31.0 1.3 %shard_map.54 = (bf16[8,128,128]{2,1,0:T(8,128)(2,1)S(1)}, f32[8,128,128]{2,1,0:T(8,128)S(1)}) custom-call(s32[8,128]{1,0:T(8,128)S(4)} %get-tuple-element.19.refs_0_, bf16[256,128,128]{2,1,0:T(8,128)(2,1)S(1)} %get-tuple-element.20.refs_1_, bf16[8,128,128]{2,1,0:T(8,128)(2,1)S(1)} %add_convert_fusion.1.refs_2_, ...), custom_call_target="tpu_custom_call" | custom-call | tf_op jit(solution)/shard_map/pallas_call | solution.py:119
  32.3 1.4 %collective-permute-start.12 = (bf16[8,128,128]{2,1,0:T(8,128)(2,1)S(1)}, bf16[8,128,128]{2,1,0:T(8,128)(2,1)S(1)}, u32[]{:S(2)}, u32[]{:S(2)}) collective-permute-start(bf16[8,128,128]{2,1,0:T(8,128)(2,1)S(1)} %get-tuple-element.31), channel_id=1, source_target_pairs={{0,4},{4,0},{8,12},{12,8},{16,24},{20,28},{24,16},{28,20},{1,5},{5... | collective-permute-start | bytes 786440 | tf_op jit(solution)/shard_map/ppermute | solution.py:170
  33.7 1.3 %shard_map.51 = (bf16[8,128,128]{2,1,0:T(8,128)(2,1)S(1)}, f32[8,128,128]{2,1,0:T(8,128)S(1)}) custom-call(s32[8,128]{1,0:T(8,128)S(4)} %get-tuple-element.19.refs_0_, bf16[256,128,128]{2,1,0:T(8,128)(2,1)S(1)} %get-tuple-element.20.refs_1_, bf16[8,128,128]{2,1,0:T(8,128)(2,1)S(1)} %add_convert_fusion.4.refs_2_, ...), custom_call_target="tpu_custom_call" | custom-call | tf_op jit(solution)/shard_map/pallas_call | solution.py:119
  35.8 1.6 %collective-permute-start.14 = (bf16[8,128,128]{2,1,0:T(8,128)(2,1)S(1)}, bf16[8,128,128]{2,1,0:T(8,128)(2,1)S(1)}, u32[]{:S(2)}, u32[]{:S(2)}) collective-permute-start(bf16[8,128,128]{2,1,0:T(8,128)(2,1)S(1)} %add_convert_fusion), channel_id=1, source_target_pairs={{0,8},{4,12},{8,0},{12,4},{16,20},{20,16},{24,28},{28,24},{1,9},{5... | collective-permute-start | bytes 786440 | tf_op jit(solution)/shard_map/ppermute | solution.py:170
  37.5 1.4 %collective-permute-start.7 = (bf16[8,128,128]{2,1,0:T(8,128)(2,1)S(1)}, bf16[8,128,128]{2,1,0:T(8,128)(2,1)S(1)}, u32[]{:S(2)}, u32[]{:S(2)}) collective-permute-start(bf16[8,128,128]{2,1,0:T(8,128)(2,1)S(1)} %add_convert_fusion.3), channel_id=1, source_target_pairs={{0,8},{4,12},{8,0},{12,4},{16,20},{20,16},{24,28},{28,24},{1,9},{5... | collective-permute-start | bytes 786440 | tf_op jit(solution)/shard_map/ppermute | solution.py:170
  40.3 0.8 %collective-permute-done.12.near = bf16[8,128,128]{2,1,0:T(8,128)(2,1)S(1)} collective-permute-done((bf16[8,128,128]{2,1,0:T(8,128)(2,1)S(1)}, bf16[8,128,128]{2,1,0:T(8,128)(2,1)S(1)}, u32[]{:S(2)}, u32[]{:S(2)}) %collective-permute-start.12) | collective-permute-done | bytes 262176 | tf_op jit(solution)/shard_map/ppermute | solution.py:170
  41.2 3.8 %collective-permute-done.14.last = bf16[8,128,128]{2,1,0:T(8,128)(2,1)S(1)} collective-permute-done((bf16[8,128,128]{2,1,0:T(8,128)(2,1)S(1)}, bf16[8,128,128]{2,1,0:T(8,128)(2,1)S(1)}, u32[]{:S(2)}, u32[]{:S(2)}) %collective-permute-start.14) | collective-permute-done | bytes 262176 | tf_op jit(solution)/shard_map/ppermute | solution.py:170
  44.9 0.8 %shard_map.56.refs_0_ = bf16[1024,256]{1,0:T(8,128)(2,1)} custom-call(f32[8,128,128]{2,1,0:T(8,128)S(1)} %shard_map.53.own, bf16[8,128,128]{2,1,0:T(8,128)(2,1)S(1)} %collective-permute-done.12.near, bf16[8,128,128]{2,1,0:T(8,128)(2,1)S(1)} %collective-permute-done.14.last), custom_call_target="tpu_custom_call" | custom-call | tf_op jit(solution)/shard_map/pallas_call | solution.py:149
  45.7 1.1 %collective-permute-done.5.near = bf16[8,128,128]{2,1,0:T(8,128)(2,1)S(1)} collective-permute-done((bf16[8,128,128]{2,1,0:T(8,128)(2,1)S(1)}, bf16[8,128,128]{2,1,0:T(8,128)(2,1)S(1)}, u32[]{:S(2)}, u32[]{:S(2)}) %collective-permute-start.5) | collective-permute-done | bytes 262176 | tf_op jit(solution)/shard_map/ppermute | solution.py:170
  46.8 1.0 %collective-permute-done.7.last = bf16[8,128,128]{2,1,0:T(8,128)(2,1)S(1)} collective-permute-done((bf16[8,128,128]{2,1,0:T(8,128)(2,1)S(1)}, bf16[8,128,128]{2,1,0:T(8,128)(2,1)S(1)}, u32[]{:S(2)}, u32[]{:S(2)}) %collective-permute-start.7) | collective-permute-done | bytes 262176 | tf_op jit(solution)/shard_map/ppermute | solution.py:170
  (26 shorter events, 6.3 us)
Async XLA Ops:
  0.0 4.7 %copy-start = (bf16[1024,256]{1,0:T(8,128)(2,1)S(1)}, bf16[1024,256]{1,0:T(8,128)(2,1)}, u32[]{:S(2)}) copy-start(bf16[1024,256]{1,0:T(8,128)(2,1)} %param.4) | copy-start | bytes 1572868
  0.0 4.6 %collective-permute-start = (bf16[8,128,256]{2,1,0:T(8,128)(2,1)}, bf16[8,128,256]{2,1,0:T(8,128)(2,1)S(1)}, u32[]{:S(2)}, u32[]{:S(2)}) collective-permute-start(bf16[8,128,256]{2,1,0:T(8,128)(2,1)} %bitcast.5), channel_id=1, source_target_pairs={{0,16},{16,0},{1,17},{17,1},{2,18},{18,2},{3,19},{19,3},{4,20},{20... | collective-permute-start | bytes 1572872 | tf_op jit(solution)/shard_map/ppermute | solution.py:175
  5.5 7.0 %collective-permute-start.9 = (bf16[8,128,128]{2,1,0:T(8,128)(2,1)S(1)}, bf16[8,128,128]{2,1,0:T(8,128)(2,1)S(1)}, u32[]{:S(2)}, u32[]{:S(2)}) collective-permute-start(bf16[8,128,128]{2,1,0:T(8,128)(2,1)S(1)} %get-tuple-element.30), channel_id=1, source_target_pairs={{0,4},{4,0},{8,12},{12,8},{16,24},{20,28},{24,16},{28,20},{1,5},{5... | collective-permute-start | bytes 786440 | tf_op jit(solution)/shard_map/ppermute | solution.py:170
  8.1 8.0 %collective-permute-start.2 = (bf16[8,128,128]{2,1,0:T(8,128)(2,1)S(1)}, bf16[8,128,128]{2,1,0:T(8,128)(2,1)S(1)}, u32[]{:S(2)}, u32[]{:S(2)}) collective-permute-start(bf16[8,128,128]{2,1,0:T(8,128)(2,1)S(1)} %get-tuple-element.24), channel_id=1, source_target_pairs={{0,4},{4,0},{8,12},{12,8},{16,24},{20,28},{24,16},{28,20},{1,5},{5... | collective-permute-start | bytes 786440 | tf_op jit(solution)/shard_map/ppermute | solution.py:170
  9.6 11.4 %collective-permute-start.8 = (bf16[8,128,128]{2,1,0:T(8,128)(2,1)S(1)}, bf16[8,128,128]{2,1,0:T(8,128)(2,1)S(1)}, u32[]{:S(2)}, u32[]{:S(2)}) collective-permute-start(bf16[8,128,128]{2,1,0:T(8,128)(2,1)S(1)} %get-tuple-element.28), channel_id=1, source_target_pairs={{0,4},{4,0},{8,12},{12,8},{16,24},{20,28},{24,16},{28,20},{1,5},{5... | collective-permute-start | bytes 786440 | tf_op jit(solution)/shard_map/ppermute | solution.py:170
  12.5 9.3 %collective-permute-start.10 = (bf16[8,128,128]{2,1,0:T(8,128)(2,1)S(1)}, bf16[8,128,128]{2,1,0:T(8,128)(2,1)S(1)}, u32[]{:S(2)}, u32[]{:S(2)}) collective-permute-start(bf16[8,128,128]{2,1,0:T(8,128)(2,1)S(1)} %add_convert_fusion.2), channel_id=1, source_target_pairs={{0,8},{4,12},{8,0},{12,4},{16,20},{20,16},{24,28},{28,24},{1,9},{5... | collective-permute-start | bytes 786440 | tf_op jit(solution)/shard_map/ppermute | solution.py:170
  14.6 11.9 %collective-permute-start.1 = (bf16[8,128,128]{2,1,0:T(8,128)(2,1)S(1)}, bf16[8,128,128]{2,1,0:T(8,128)(2,1)S(1)}, u32[]{:S(2)}, u32[]{:S(2)}) collective-permute-start(bf16[8,128,128]{2,1,0:T(8,128)(2,1)S(1)} %get-tuple-element.22), channel_id=1, source_target_pairs={{0,4},{4,0},{8,12},{12,8},{16,24},{20,28},{24,16},{28,20},{1,5},{5... | collective-permute-start | bytes 786440 | tf_op jit(solution)/shard_map/ppermute | solution.py:170
  16.2 10.3 %collective-permute-start.3 = (bf16[8,128,128]{2,1,0:T(8,128)(2,1)S(1)}, bf16[8,128,128]{2,1,0:T(8,128)(2,1)S(1)}, u32[]{:S(2)}, u32[]{:S(2)}) collective-permute-start(bf16[8,128,128]{2,1,0:T(8,128)(2,1)S(1)} %add_convert_fusion.5), channel_id=1, source_target_pairs={{0,8},{4,12},{8,0},{12,4},{16,20},{20,16},{24,28},{28,24},{1,9},{5... | collective-permute-start | bytes 786440 | tf_op jit(solution)/shard_map/ppermute | solution.py:170
  22.0 4.7 %collective-permute-start.11 = (bf16[8,128,128]{2,1,0:T(8,128)(2,1)S(1)}, bf16[8,128,128]{2,1,0:T(8,128)(2,1)S(1)}, u32[]{:S(2)}, u32[]{:S(2)}) collective-permute-start(bf16[8,128,128]{2,1,0:T(8,128)(2,1)S(1)} %add_convert_fusion.1.refs_2_), channel_id=1, source_target_pairs={{0,16},{16,0},{1,17},{17,1},{2,18},{18,2},{3,19},{19,3},{4,20},{20... | collective-permute-start | bytes 786440 | tf_op jit(solution)/shard_map/ppermute | solution.py:175
  26.6 2.9 %collective-permute-start.4 = (bf16[8,128,128]{2,1,0:T(8,128)(2,1)S(1)}, bf16[8,128,128]{2,1,0:T(8,128)(2,1)S(1)}, u32[]{:S(2)}, u32[]{:S(2)}) collective-permute-start(bf16[8,128,128]{2,1,0:T(8,128)(2,1)S(1)} %add_convert_fusion.4.refs_2_), channel_id=1, source_target_pairs={{0,16},{16,0},{1,17},{17,1},{2,18},{18,2},{3,19},{19,3},{4,20},{20... | collective-permute-start | bytes 786440 | tf_op jit(solution)/shard_map/ppermute | solution.py:175
  27.4 8.3 %collective-permute-start.13 = (bf16[8,128,128]{2,1,0:T(8,128)(2,1)S(1)}, bf16[8,128,128]{2,1,0:T(8,128)(2,1)S(1)}, u32[]{:S(2)}, u32[]{:S(2)}) collective-permute-start(bf16[8,128,128]{2,1,0:T(8,128)(2,1)S(1)} %shard_map.55), channel_id=1, source_target_pairs={{0,4},{4,0},{8,12},{12,8},{16,24},{20,28},{24,16},{28,20},{1,5},{5... | collective-permute-start | bytes 786440 | tf_op jit(solution)/shard_map/ppermute | solution.py:170
  30.3 7.1 %collective-permute-start.6 = (bf16[8,128,128]{2,1,0:T(8,128)(2,1)S(1)}, bf16[8,128,128]{2,1,0:T(8,128)(2,1)S(1)}, u32[]{:S(2)}, u32[]{:S(2)}) collective-permute-start(bf16[8,128,128]{2,1,0:T(8,128)(2,1)S(1)} %shard_map.52), channel_id=1, source_target_pairs={{0,4},{4,0},{8,12},{12,8},{16,24},{20,28},{24,16},{28,20},{1,5},{5... | collective-permute-start | bytes 786440 | tf_op jit(solution)/shard_map/ppermute | solution.py:170
  32.3 8.9 %collective-permute-start.12 = (bf16[8,128,128]{2,1,0:T(8,128)(2,1)S(1)}, bf16[8,128,128]{2,1,0:T(8,128)(2,1)S(1)}, u32[]{:S(2)}, u32[]{:S(2)}) collective-permute-start(bf16[8,128,128]{2,1,0:T(8,128)(2,1)S(1)} %get-tuple-element.31), channel_id=1, source_target_pairs={{0,4},{4,0},{8,12},{12,8},{16,24},{20,28},{24,16},{28,20},{1,5},{5... | collective-permute-start | bytes 786440 | tf_op jit(solution)/shard_map/ppermute | solution.py:170
  35.0 11.8 %collective-permute-start.5 = (bf16[8,128,128]{2,1,0:T(8,128)(2,1)S(1)}, bf16[8,128,128]{2,1,0:T(8,128)(2,1)S(1)}, u32[]{:S(2)}, u32[]{:S(2)}) collective-permute-start(bf16[8,128,128]{2,1,0:T(8,128)(2,1)S(1)} %get-tuple-element.25), channel_id=1, source_target_pairs={{0,4},{4,0},{8,12},{12,8},{16,24},{20,28},{24,16},{28,20},{1,5},{5... | collective-permute-start | bytes 786440 | tf_op jit(solution)/shard_map/ppermute | solution.py:170
  35.8 9.1 %collective-permute-start.14 = (bf16[8,128,128]{2,1,0:T(8,128)(2,1)S(1)}, bf16[8,128,128]{2,1,0:T(8,128)(2,1)S(1)}, u32[]{:S(2)}, u32[]{:S(2)}) collective-permute-start(bf16[8,128,128]{2,1,0:T(8,128)(2,1)S(1)} %add_convert_fusion), channel_id=1, source_target_pairs={{0,8},{4,12},{8,0},{12,4},{16,20},{20,16},{24,28},{28,24},{1,9},{5... | collective-permute-start | bytes 786440 | tf_op jit(solution)/shard_map/ppermute | solution.py:170
  37.5 10.3 %collective-permute-start.7 = (bf16[8,128,128]{2,1,0:T(8,128)(2,1)S(1)}, bf16[8,128,128]{2,1,0:T(8,128)(2,1)S(1)}, u32[]{:S(2)}, u32[]{:S(2)}) collective-permute-start(bf16[8,128,128]{2,1,0:T(8,128)(2,1)S(1)} %add_convert_fusion.3), channel_id=1, source_target_pairs={{0,8},{4,12},{8,0},{12,4},{16,20},{20,16},{24,28},{28,24},{1,9},{5... | collective-permute-start | bytes 786440 | tf_op jit(solution)/shard_map/ppermute | solution.py:170

commit v5 on v4

--- a/solution.py
+++ b/solution.py
@@ -193,9 +193,9 @@
     def couple(source):
         (far,) = sweep(table, tiles, source, 0, [(share, bf16)])
         far = [first(f) for f in far]
-        near, kept = sweep(table, tiles, source, share, [(share, bf16), (share, f32)])
+        (near,) = sweep(table, tiles, source, share, [(share, bf16)])
         near = [first(n) for n in near]
-        (own,) = sweep(table, tiles, source, 3 * share, [(share, f32)])
+        kept, own = sweep(table, tiles, source, 2 * share, [(share, f32), (share, f32)])
         last = [second((k + f.astype(f32)).astype(bf16)) for k, f in zip(kept, far)]
         return list(zip(own, near, last))
 

time: 48.7 us -> 48.7 us (level)
  starting transfers between devices: 18.6 us -> 17.7 us
  waiting for transfers between devices: 15.1 us -> 15.9 us
    ppermute x12, starting transfers between devices: 18 us -> 17.2 us  [exchange(): return lax.ppermute(values, ('row', 'col'), pairs)]
    ppermute x12, waiting for transfers between devices: 15.1 us -> 15.9 us  [exchange(): return lax.ppermute(values, ('row', 'col'), pairs)]
  transfers between devices with their start and end apart: 15 -> 15, of which waited for: 8 -> 5; matrix products, arithmetic and copies ran while one was open for 1% -> 1% of each run, Pallas kernels for 25% -> 25%
where the time goes in v5:
time: 48.7 us; the launch traced here: 48.5 us
  starting transfers between devices  17.7 us (36%)
  waiting for transfers between devices  15.9 us (33%)
  Pallas kernels  13.6 us (28%)
  between operations  0.82 us (2%)
    ppermute x12, starting transfers between devices, exchange(): return lax.ppermute(values, ('row', 'col'), pairs)  17.2 us
    ppermute x12, waiting for transfers between devices, exchange(): return lax.ppermute(values, ('row', 'col'), pairs)  15.9 us
    pallas_call x9, Pallas kernels, sweep(): pl.pallas_call(functools.partial(sweep_kernel, [n for n, _ in outs], firs...  8.53 us
    pallas_call x1, Pallas kernels, load(): pl.pallas_call(functools.partial(load_kernel, own_first, share, blocks),...  3.53 us
    pallas_call x2, Pallas kernels, finish(): pl.pallas_call(functools.partial(finish_kernel, column), out_shape=pltpu....  1.54 us
  transfers between devices with their start and end apart: 15, of which 5 were waited for; matrix products, arithmetic and copies ran while one was open for 1% of the time, Pallas kernels for 25%

profile of v5, /device:TPU:0, one launch (start us, length us, event | category | flops | bytes accessed | tf_op | source)
XLA Modules:
  0.0 48.5 jit_solution(2856202888411870566)
XLA Ops:
  1.1 3.5 %shard_map.46 = (s32[8,128]{1,0:T(8,128)S(4)}, bf16[256,128,128]{2,1,0:T(8,128)(2,1)S(1)}) custom-call(s32[2,256]{1,0:T(2,128)} %bitcast.10, s32[1,1]{1,0:T(1,128)S(6)} %copy.7.count, bf16[256,128,128]{2,1,0:T(8,128)(2,1)} %bitcast.9), custom_call_target="tpu_custom_call" | custom-call | tf_op jit(solution)/shard_map/pallas_call | solution.py:68
  4.7 0.8 %shard_map.49 = (bf16[8,128,128]{2,1,0:T(8,128)(2,1)S(1)}, bf16[8,128,128]{2,1,0:T(8,128)(2,1)S(1)}) custom-call(s32[8,128]{1,0:T(8,128)S(4)} %get-tuple-element.19.refs_0_, bf16[256,128,128]{2,1,0:T(8,128)(2,1)S(1)} %get-tuple-element.20.refs_1_, bf16[8,128,256]{2,1,0:T(8,128)(2,1)S(1)} %bitcast.6, bf16[8,128,256]{2,1,0:T(8,128)(2,1)S(1)} %collective-permute-done.refs_3_), custom_call_target="tpu_custom_call" | custom-call | tf_op jit(solution)/shard_map/pallas_call | solution.py:119
  5.5 2.6 %collective-permute-start.9 = (bf16[8,128,128]{2,1,0:T(8,128)(2,1)S(1)}, bf16[8,128,128]{2,1,0:T(8,128)(2,1)S(1)}, u32[]{:S(2)}, u32[]{:S(2)}) collective-permute-start(bf16[8,128,128]{2,1,0:T(8,128)(2,1)S(1)} %get-tuple-element.30), channel_id=1, source_target_pairs={{0,4},{4,0},{8,12},{12,8},{16,24},{20,28},{24,16},{28,20},{1,5},{5... | collective-permute-start | bytes 786440 | tf_op jit(solution)/shard_map/ppermute | solution.py:170
  8.2 0.8 %shard_map.48 = (bf16[8,128,128]{2,1,0:T(8,128)(2,1)S(1)}, bf16[8,128,128]{2,1,0:T(8,128)(2,1)S(1)}) custom-call(s32[8,128]{1,0:T(8,128)S(4)} %get-tuple-element.19.refs_0_, bf16[256,128,128]{2,1,0:T(8,128)(2,1)S(1)} %get-tuple-element.20.refs_1_, bf16[8,128,256]{2,1,0:T(8,128)(2,1)S(1)} %bitcast.7, bf16[8,128,256]{2,1,0:T(8,128)(2,1)S(1)} %collective-permute-done.refs_3_), custom_call_target="tpu_custom_call" | custom-call | tf_op jit(solution)/shard_map/pallas_call | solution.py:119
  9.0 2.0 %collective-permute-start.8 = (bf16[8,128,128]{2,1,0:T(8,128)(2,1)S(1)}, bf16[8,128,128]{2,1,0:T(8,128)(2,1)S(1)}, u32[]{:S(2)}, u32[]{:S(2)}) collective-permute-start(bf16[8,128,128]{2,1,0:T(8,128)(2,1)S(1)} %get-tuple-element.28), channel_id=1, source_target_pairs={{0,4},{4,0},{8,12},{12,8},{16,24},{20,28},{24,16},{28,20},{1,5},{5... | collective-permute-start | bytes 786440 | tf_op jit(solution)/shard_map/ppermute | solution.py:170
  11.0 1.4 %shard_map.47 = (f32[8,128,128]{2,1,0:T(8,128)S(1)}, f32[8,128,128]{2,1,0:T(8,128)S(1)}, f32[8,128,128]{2,1,0:T(8,128)S(1)}, f32[8,128,128]{2,1,0:T(8,128)S(1)}) custom-call(s32[8,128]{1,0:T(8,128)S(4)} %get-tuple-element.19.refs_0_, bf16[256,128,128]{2,1,0:T(8,128)(2,1)S(1)} %get-tuple-element.20.refs_1_, bf16[8,128,256]{2,1,0:T(8,128)(2,1)S(1)} %bitcast.8, ...), custom_call_target="tpu_custom_call" | custom-call | tf_op jit(solution)/shard_map/pallas_call | solution.py:119
  12.5 2.1 %collective-permute-start.10 = (bf16[8,128,128]{2,1,0:T(8,128)(2,1)S(1)}, bf16[8,128,128]{2,1,0:T(8,128)(2,1)S(1)}, u32[]{:S(2)}, u32[]{:S(2)}) collective-permute-start(bf16[8,128,128]{2,1,0:T(8,128)(2,1)S(1)} %add_convert_fusion.2), channel_id=1, source_target_pairs={{0,8},{4,12},{8,0},{12,4},{16,20},{20,16},{24,28},{28,24},{1,9},{5... | collective-permute-start | bytes 786440 | tf_op jit(solution)/shard_map/ppermute | solution.py:170
  14.6 1.5 %collective-permute-start.1 = (bf16[8,128,128]{2,1,0:T(8,128)(2,1)S(1)}, bf16[8,128,128]{2,1,0:T(8,128)(2,1)S(1)}, u32[]{:S(2)}, u32[]{:S(2)}) collective-permute-start(bf16[8,128,128]{2,1,0:T(8,128)(2,1)S(1)} %get-tuple-element.22), channel_id=1, source_target_pairs={{0,4},{4,0},{8,12},{12,8},{16,24},{20,28},{24,16},{28,20},{1,5},{5... | collective-permute-start | bytes 786440 | tf_op jit(solution)/shard_map/ppermute | solution.py:170
  16.2 1.7 %collective-permute-start.3 = (bf16[8,128,128]{2,1,0:T(8,128)(2,1)S(1)}, bf16[8,128,128]{2,1,0:T(8,128)(2,1)S(1)}, u32[]{:S(2)}, u32[]{:S(2)}) collective-permute-start(bf16[8,128,128]{2,1,0:T(8,128)(2,1)S(1)} %add_convert_fusion.5), channel_id=1, source_target_pairs={{0,8},{4,12},{8,0},{12,4},{16,20},{20,16},{24,28},{28,24},{1,9},{5... | collective-permute-start | bytes 786440 | tf_op jit(solution)/shard_map/ppermute | solution.py:170
  17.9 3.1 %collective-permute-done.8 = bf16[8,128,128]{2,1,0:T(8,128)(2,1)S(1)} collective-permute-done((bf16[8,128,128]{2,1,0:T(8,128)(2,1)S(1)}, bf16[8,128,128]{2,1,0:T(8,128)(2,1)S(1)}, u32[]{:S(2)}, u32[]{:S(2)}) %collective-permute-start.8) | collective-permute-done | bytes 262176 | tf_op jit(solution)/shard_map/ppermute | solution.py:170
  21.0 0.9 %collective-permute-done.10 = bf16[8,128,128]{2,1,0:T(8,128)(2,1)S(1)} collective-permute-done((bf16[8,128,128]{2,1,0:T(8,128)(2,1)S(1)}, bf16[8,128,128]{2,1,0:T(8,128)(2,1)S(1)}, u32[]{:S(2)}, u32[]{:S(2)}) %collective-permute-start.10) | collective-permute-done | bytes 262176 | tf_op jit(solution)/shard_map/ppermute | solution.py:170
  22.0 4.5 %collective-permute-done.1 = bf16[8,128,128]{2,1,0:T(8,128)(2,1)S(1)} collective-permute-done((bf16[8,128,128]{2,1,0:T(8,128)(2,1)S(1)}, bf16[8,128,128]{2,1,0:T(8,128)(2,1)S(1)}, u32[]{:S(2)}, u32[]{:S(2)}) %collective-permute-start.1) | collective-permute-done | bytes 262176 | tf_op jit(solution)/shard_map/ppermute | solution.py:170
  26.7 0.7 %shard_map.55 = bf16[8,128,128]{2,1,0:T(8,128)(2,1)S(1)} custom-call(s32[8,128]{1,0:T(8,128)S(4)} %get-tuple-element.19.refs_0_, bf16[256,128,128]{2,1,0:T(8,128)(2,1)S(1)} %get-tuple-element.20.refs_1_, bf16[8,128,128]{2,1,0:T(8,128)(2,1)S(1)} %add_convert_fusion.1.refs_2_, bf16[8,128,128]{2,1,0:T(8,128)(2,1)S(1)} %collective-permute-done.11.refs_3_), custom_call_target="tpu_custom_call" | custom-call | tf_op jit(solution)/shard_map/pallas_call | solution.py:119
  27.4 2.1 %collective-permute-start.13 = (bf16[8,128,128]{2,1,0:T(8,128)(2,1)S(1)}, bf16[8,128,128]{2,1,0:T(8,128)(2,1)S(1)}, u32[]{:S(2)}, u32[]{:S(2)}) collective-permute-start(bf16[8,128,128]{2,1,0:T(8,128)(2,1)S(1)} %shard_map.55), channel_id=1, source_target_pairs={{0,4},{4,0},{8,12},{12,8},{16,24},{20,28},{24,16},{28,20},{1,5},{5... | collective-permute-start | bytes 786440 | tf_op jit(solution)/shard_map/ppermute | solution.py:170
  30.3 0.8 %collective-permute-start.6 = (bf16[8,128,128]{2,1,0:T(8,128)(2,1)S(1)}, bf16[8,128,128]{2,1,0:T(8,128)(2,1)S(1)}, u32[]{:S(2)}, u32[]{:S(2)}) collective-permute-start(bf16[8,128,128]{2,1,0:T(8,128)(2,1)S(1)} %shard_map.52), channel_id=1, source_target_pairs={{0,4},{4,0},{8,12},{12,8},{16,24},{20,28},{24,16},{28,20},{1,5},{5... | collective-permute-start | bytes 786440 | tf_op jit(solution)/shard_map/ppermute | solution.py:170
  31.8 1.4 %collective-permute-start.5 = (bf16[8,128,128]{2,1,0:T(8,128)(2,1)S(1)}, bf16[8,128,128]{2,1,0:T(8,128)(2,1)S(1)}, u32[]{:S(2)}, u32[]{:S(2)}) collective-permute-start(bf16[8,128,128]{2,1,0:T(8,128)(2,1)S(1)} %shard_map.51), channel_id=1, source_target_pairs={{0,4},{4,0},{8,12},{12,8},{16,24},{20,28},{24,16},{28,20},{1,5},{5... | collective-permute-start | bytes 786440 | tf_op jit(solution)/shard_map/ppermute | solution.py:170
  33.9 0.8 %collective-permute-start.12 = (bf16[8,128,128]{2,1,0:T(8,128)(2,1)S(1)}, bf16[8,128,128]{2,1,0:T(8,128)(2,1)S(1)}, u32[]{:S(2)}, u32[]{:S(2)}) collective-permute-start(bf16[8,128,128]{2,1,0:T(8,128)(2,1)S(1)} %shard_map.54), channel_id=1, source_target_pairs={{0,4},{4,0},{8,12},{12,8},{16,24},{20,28},{24,16},{28,20},{1,5},{5... | collective-permute-start | bytes 786440 | tf_op jit(solution)/shard_map/ppermute | solution.py:170
  34.7 1.3 %shard_map.53 = (f32[8,128,128]{2,1,0:T(8,128)S(1)}, f32[8,128,128]{2,1,0:T(8,128)S(1)}) custom-call(s32[8,128]{1,0:T(8,128)S(4)} %get-tuple-element.19.refs_0_, bf16[256,128,128]{2,1,0:T(8,128)(2,1)S(1)} %get-tuple-element.20.refs_1_, bf16[8,128,128]{2,1,0:T(8,128)(2,1)S(1)} %add_convert_fusion.1.refs_2_, ...), custom_call_target="tpu_custom_call" | custom-call | tf_op jit(solution)/shard_map/pallas_call | solution.py:119
  36.0 1.3 %shard_map.50 = (f32[8,128,128]{2,1,0:T(8,128)S(1)}, f32[8,128,128]{2,1,0:T(8,128)S(1)}) custom-call(s32[8,128]{1,0:T(8,128)S(4)} %get-tuple-element.19.refs_0_, bf16[256,128,128]{2,1,0:T(8,128)(2,1)S(1)} %get-tuple-element.20.refs_1_, bf16[8,128,128]{2,1,0:T(8,128)(2,1)S(1)} %add_convert_fusion.4.refs_2_, ...), custom_call_target="tpu_custom_call" | custom-call | tf_op jit(solution)/shard_map/pallas_call | solution.py:119
  37.3 1.6 %collective-permute-start.14 = (bf16[8,128,128]{2,1,0:T(8,128)(2,1)S(1)}, bf16[8,128,128]{2,1,0:T(8,128)(2,1)S(1)}, u32[]{:S(2)}, u32[]{:S(2)}) collective-permute-start(bf16[8,128,128]{2,1,0:T(8,128)(2,1)S(1)} %add_convert_fusion), channel_id=1, source_target_pairs={{0,8},{4,12},{8,0},{12,4},{16,20},{20,16},{24,28},{28,24},{1,9},{5... | collective-permute-start | bytes 786440 | tf_op jit(solution)/shard_map/ppermute | solution.py:170
  39.5 5.8 %collective-permute-done.12.near = bf16[8,128,128]{2,1,0:T(8,128)(2,1)S(1)} collective-permute-done((bf16[8,128,128]{2,1,0:T(8,128)(2,1)S(1)}, bf16[8,128,128]{2,1,0:T(8,128)(2,1)S(1)}, u32[]{:S(2)}, u32[]{:S(2)}) %collective-permute-start.12) | collective-permute-done | bytes 262176 | tf_op jit(solution)/shard_map/ppermute | solution.py:170
  45.3 0.8 %shard_map.56.refs_0_ = bf16[1024,256]{1,0:T(8,128)(2,1)} custom-call(f32[8,128,128]{2,1,0:T(8,128)S(1)} %get-tuple-element.31.own, bf16[8,128,128]{2,1,0:T(8,128)(2,1)S(1)} %collective-permute-done.12.near, bf16[8,128,128]{2,1,0:T(8,128)(2,1)S(1)} %collective-permute-done.14.last), custom_call_target="tpu_custom_call" | custom-call | tf_op jit(solution)/shard_map/pallas_call | solution.py:149
  46.1 1.7 %collective-permute-done.7.last = bf16[8,128,128]{2,1,0:T(8,128)(2,1)S(1)} collective-permute-done((bf16[8,128,128]{2,1,0:T(8,128)(2,1)S(1)}, bf16[8,128,128]{2,1,0:T(8,128)(2,1)S(1)}, u32[]{:S(2)}, u32[]{:S(2)}) %collective-permute-start.7) | collective-permute-done | bytes 262176 | tf_op jit(solution)/shard_map/ppermute | solution.py:170
  47.8 0.8 %shard_map.57 = bf16[1024,256]{1,0:T(8,128)(2,1)} custom-call(f32[8,128,128]{2,1,0:T(8,128)S(1)} %get-tuple-element.25.own, bf16[8,128,128]{2,1,0:T(8,128)(2,1)S(1)} %collective-permute-done.5.near, bf16[8,128,128]{2,1,0:T(8,128)(2,1)S(1)} %collective-permute-done.7.last, bf16[1024,256]{1,0:T(8,128)(2,1)} %shard_map.56.refs_0_), custom_call_target="tpu_custom_call", output_to_operand_aliasing={{}: (3, {})} | custom-call | tf_op jit(solution)/shard_map/pallas_call | solution.py:149
  (26 shorter events, 3.9 us)
Async XLA Ops:
  0.0 4.7 %copy-start = (bf16[1024,256]{1,0:T(8,128)(2,1)S(1)}, bf16[1024,256]{1,0:T(8,128)(2,1)}, u32[]{:S(2)}) copy-start(bf16[1024,256]{1,0:T(8,128)(2,1)} %param.4) | copy-start | bytes 1572868
  0.0 4.6 %collective-permute-start = (bf16[8,128,256]{2,1,0:T(8,128)(2,1)}, bf16[8,128,256]{2,1,0:T(8,128)(2,1)S(1)}, u32[]{:S(2)}, u32[]{:S(2)}) collective-permute-start(bf16[8,128,256]{2,1,0:T(8,128)(2,1)} %bitcast.5), channel_id=1, source_target_pairs={{0,16},{16,0},{1,17},{17,1},{2,18},{18,2},{3,19},{19,3},{4,20},{20... | collective-permute-start | bytes 1572872 | tf_op jit(solution)/shard_map/ppermute | solution.py:175
  5.5 7.0 %collective-permute-start.9 = (bf16[8,128,128]{2,1,0:T(8,128)(2,1)S(1)}, bf16[8,128,128]{2,1,0:T(8,128)(2,1)S(1)}, u32[]{:S(2)}, u32[]{:S(2)}) collective-permute-start(bf16[8,128,128]{2,1,0:T(8,128)(2,1)S(1)} %get-tuple-element.30), channel_id=1, source_target_pairs={{0,4},{4,0},{8,12},{12,8},{16,24},{20,28},{24,16},{28,20},{1,5},{5... | collective-permute-start | bytes 786440 | tf_op jit(solution)/shard_map/ppermute | solution.py:170
  8.1 8.0 %collective-permute-start.2 = (bf16[8,128,128]{2,1,0:T(8,128)(2,1)S(1)}, bf16[8,128,128]{2,1,0:T(8,128)(2,1)S(1)}, u32[]{:S(2)}, u32[]{:S(2)}) collective-permute-start(bf16[8,128,128]{2,1,0:T(8,128)(2,1)S(1)} %get-tuple-element.24), channel_id=1, source_target_pairs={{0,4},{4,0},{8,12},{12,8},{16,24},{20,28},{24,16},{28,20},{1,5},{5... | collective-permute-start | bytes 786440 | tf_op jit(solution)/shard_map/ppermute | solution.py:170
  9.0 12.0 %collective-permute-start.8 = (bf16[8,128,128]{2,1,0:T(8,128)(2,1)S(1)}, bf16[8,128,128]{2,1,0:T(8,128)(2,1)S(1)}, u32[]{:S(2)}, u32[]{:S(2)}) collective-permute-start(bf16[8,128,128]{2,1,0:T(8,128)(2,1)S(1)} %get-tuple-element.28), channel_id=1, source_target_pairs={{0,4},{4,0},{8,12},{12,8},{16,24},{20,28},{24,16},{28,20},{1,5},{5... | collective-permute-start | bytes 786440 | tf_op jit(solution)/shard_map/ppermute | solution.py:170
  12.5 9.3 %collective-permute-start.10 = (bf16[8,128,128]{2,1,0:T(8,128)(2,1)S(1)}, bf16[8,128,128]{2,1,0:T(8,128)(2,1)S(1)}, u32[]{:S(2)}, u32[]{:S(2)}) collective-permute-start(bf16[8,128,128]{2,1,0:T(8,128)(2,1)S(1)} %add_convert_fusion.2), channel_id=1, source_target_pairs={{0,8},{4,12},{8,0},{12,4},{16,20},{20,16},{24,28},{28,24},{1,9},{5... | collective-permute-start | bytes 786440 | tf_op jit(solution)/shard_map/ppermute | solution.py:170
  14.6 11.9 %collective-permute-start.1 = (bf16[8,128,128]{2,1,0:T(8,128)(2,1)S(1)}, bf16[8,128,128]{2,1,0:T(8,128)(2,1)S(1)}, u32[]{:S(2)}, u32[]{:S(2)}) collective-permute-start(bf16[8,128,128]{2,1,0:T(8,128)(2,1)S(1)} %get-tuple-element.22), channel_id=1, source_target_pairs={{0,4},{4,0},{8,12},{12,8},{16,24},{20,28},{24,16},{28,20},{1,5},{5... | collective-permute-start | bytes 786440 | tf_op jit(solution)/shard_map/ppermute | solution.py:170
  16.2 10.3 %collective-permute-start.3 = (bf16[8,128,128]{2,1,0:T(8,128)(2,1)S(1)}, bf16[8,128,128]{2,1,0:T(8,128)(2,1)S(1)}, u32[]{:S(2)}, u32[]{:S(2)}) collective-permute-start(bf16[8,128,128]{2,1,0:T(8,128)(2,1)S(1)} %add_convert_fusion.5), channel_id=1, source_target_pairs={{0,8},{4,12},{8,0},{12,4},{16,20},{20,16},{24,28},{28,24},{1,9},{5... | collective-permute-start | bytes 786440 | tf_op jit(solution)/shard_map/ppermute | solution.py:170
  22.0 4.7 %collective-permute-start.11 = (bf16[8,128,128]{2,1,0:T(8,128)(2,1)S(1)}, bf16[8,128,128]{2,1,0:T(8,128)(2,1)S(1)}, u32[]{:S(2)}, u32[]{:S(2)}) collective-permute-start(bf16[8,128,128]{2,1,0:T(8,128)(2,1)S(1)} %add_convert_fusion.1.refs_2_), channel_id=1, source_target_pairs={{0,16},{16,0},{1,17},{17,1},{2,18},{18,2},{3,19},{19,3},{4,20},{20... | collective-permute-start | bytes 786440 | tf_op jit(solution)/shard_map/ppermute | solution.py:175
  26.6 2.9 %collective-permute-start.4 = (bf16[8,128,128]{2,1,0:T(8,128)(2,1)S(1)}, bf16[8,128,128]{2,1,0:T(8,128)(2,1)S(1)}, u32[]{:S(2)}, u32[]{:S(2)}) collective-permute-start(bf16[8,128,128]{2,1,0:T(8,128)(2,1)S(1)} %add_convert_fusion.4.refs_2_), channel_id=1, source_target_pairs={{0,16},{16,0},{1,17},{17,1},{2,18},{18,2},{3,19},{19,3},{4,20},{20... | collective-permute-start | bytes 786440 | tf_op jit(solution)/shard_map/ppermute | solution.py:175
  27.4 9.8 %collective-permute-start.13 = (bf16[8,128,128]{2,1,0:T(8,128)(2,1)S(1)}, bf16[8,128,128]{2,1,0:T(8,128)(2,1)S(1)}, u32[]{:S(2)}, u32[]{:S(2)}) collective-permute-start(bf16[8,128,128]{2,1,0:T(8,128)(2,1)S(1)} %shard_map.55), channel_id=1, source_target_pairs={{0,4},{4,0},{8,12},{12,8},{16,24},{20,28},{24,16},{28,20},{1,5},{5... | collective-permute-start | bytes 786440 | tf_op jit(solution)/shard_map/ppermute | solution.py:170
  30.3 8.6 %collective-permute-start.6 = (bf16[8,128,128]{2,1,0:T(8,128)(2,1)S(1)}, bf16[8,128,128]{2,1,0:T(8,128)(2,1)S(1)}, u32[]{:S(2)}, u32[]{:S(2)}) collective-permute-start(bf16[8,128,128]{2,1,0:T(8,128)(2,1)S(1)} %shard_map.52), channel_id=1, source_target_pairs={{0,4},{4,0},{8,12},{12,8},{16,24},{20,28},{24,16},{28,20},{1,5},{5... | collective-permute-start | bytes 786440 | tf_op jit(solution)/shard_map/ppermute | solution.py:170
  31.8 14.3 %collective-permute-start.5 = (bf16[8,128,128]{2,1,0:T(8,128)(2,1)S(1)}, bf16[8,128,128]{2,1,0:T(8,128)(2,1)S(1)}, u32[]{:S(2)}, u32[]{:S(2)}) collective-permute-start(bf16[8,128,128]{2,1,0:T(8,128)(2,1)S(1)} %shard_map.51), channel_id=1, source_target_pairs={{0,4},{4,0},{8,12},{12,8},{16,24},{20,28},{24,16},{28,20},{1,5},{5... | collective-permute-start | bytes 786440 | tf_op jit(solution)/shard_map/ppermute | solution.py:170
  33.9 11.4 %collective-permute-start.12 = (bf16[8,128,128]{2,1,0:T(8,128)(2,1)S(1)}, bf16[8,128,128]{2,1,0:T(8,128)(2,1)S(1)}, u32[]{:S(2)}, u32[]{:S(2)}) collective-permute-start(bf16[8,128,128]{2,1,0:T(8,128)(2,1)S(1)} %shard_map.54), channel_id=1, source_target_pairs={{0,4},{4,0},{8,12},{12,8},{16,24},{20,28},{24,16},{28,20},{1,5},{5... | collective-permute-start | bytes 786440 | tf_op jit(solution)/shard_map/ppermute | solution.py:170
  37.3 8.0 %collective-permute-start.14 = (bf16[8,128,128]{2,1,0:T(8,128)(2,1)S(1)}, bf16[8,128,128]{2,1,0:T(8,128)(2,1)S(1)}, u32[]{:S(2)}, u32[]{:S(2)}) collective-permute-start(bf16[8,128,128]{2,1,0:T(8,128)(2,1)S(1)} %add_convert_fusion), channel_id=1, source_target_pairs={{0,8},{4,12},{8,0},{12,4},{16,20},{20,16},{24,28},{28,24},{1,9},{5... | collective-permute-start | bytes 786440 | tf_op jit(solution)/shard_map/ppermute | solution.py:170
  39.0 8.8 %collective-permute-start.7 = (bf16[8,128,128]{2,1,0:T(8,128)(2,1)S(1)}, bf16[8,128,128]{2,1,0:T(8,128)(2,1)S(1)}, u32[]{:S(2)}, u32[]{:S(2)}) collective-permute-start(bf16[8,128,128]{2,1,0:T(8,128)(2,1)S(1)} %add_convert_fusion.3), channel_id=1, source_target_pairs={{0,8},{4,12},{8,0},{12,4},{16,20},{20,16},{24,28},{28,24},{1,9},{5... | collective-permute-start | bytes 786440 | tf_op jit(solution)/shard_map/ppermute | solution.py:170
